TPU v7x, 128 devices: a whole 4x4x4 slice. The times are simulated.
128 devices in a mesh: tx: 16 (over z, x), ty: 8 (over y, core).
Axes of the slice: x: 4, y: 4, z: 4, core: 2. Of those that a mesh axis runs over, the one named last changes fastest.
Arguments:
- sar_image: bfloat16 [2, 8192, 512], P(None, ('tx', 'ty')), may hold values from -6 to 6
- kernel_first: bfloat16 [16, 2, 3, 3], replicated, may hold values from -2 to 2
- kernel_second: bfloat16 [16, 16, 3, 3], replicated, may hold values from -0.75 to 0.75
- kernel_third: bfloat16 [16, 16, 3, 3], replicated, may hold values from -0.75 to 0.75
- kernel_last: bfloat16 [1, 16, 3, 3], replicated, may hold values from -1 to 1
- geo_weight: float32 [8192, 512], P(('tx', 'ty')), may hold values from 0.25 to 1
- cell_index: int32 [8192, 512], P(('tx', 'ty')), may hold values from 0 to 511
- block_tile: int32 [8192, 1], P(('tx', 'ty')), may hold values from 0 to 127; in each aligned block of 64 rows (0 to 63, 64 to 127, ...) at most 2 rows name the same one
- block_row: int32 [8192, 1], P(('tx', 'ty')), may hold values from 0 to 254
- depth: float32 [4096, 2048], P('tx', 'ty'), may hold values from 0.1 to 1
- slope: float32 [4096, 2048], P('tx', 'ty'), may hold values from 0.01 to 1
- flow_dir: int32 [4096, 2048], P('tx', 'ty'), may hold values from 0 to 7
- rain: float32 [4096, 2048], P('tx', 'ty'), may hold values from 0 to 0.1
Outputs:
- water_fraction: bfloat16 [8192, 512], P(('tx', 'ty'))
- level: float32 [4096, 2048], P('tx', 'ty')
Inputs may be any that keep to these rules, and one draw needn't show every extreme that they name: `block_tile`: in the rows of one device no tile is named more than 2 times, a bound that some block reaches.
All inputs are finite; a program needn't handle non-finite values.
Results may differ from a plain program's by a relative error of at most 0.003.
The roundings to bfloat16 on the way count: a program that leaves them out, or rounds other values in their place, can miss the bound.
Values may be sent and summed in bfloat16 or wider, within the bound.
A program may use at most 128 MiB of HBM per device.

v0:
```python
import math

import jax
import jax.numpy as jnp
from jax import lax
from jax.sharding import PartitionSpec as P

WIN_ROWS = 2
SUBSTEPS = 8


wet_depth = 0.5
runoff_coef = 0.25
neighbour_steps = ((-1, -1), (-1, 0), (-1, 1), (0, -1), (0, 1), (1, -1), (1, 0), (1, 1))


def extended(x, sides, width):
    for axis, dim in sides:
        size, length = (lax.axis_size(axis), x.shape[dim])
        up = [(i, (i + 1) % size) for i in range(size - 1)]
        down = [(j, i) for i, j in up]
        last = lax.slice_in_dim(x, length - width, length, axis=dim)
        leading = lax.slice_in_dim(x, 0, width, axis=dim)
        before = lax.ppermute(last, axis, up)
        after = lax.ppermute(leading, axis, down)
        x = jnp.concatenate([before, x, after], axis=dim)
    return x


def conv_rows(activation, kernel):
    result = lax.conv_general_dilated(
        activation[None],
        kernel,
        (1, 1),
        ((0, 0), (1, 1)),
        dimension_numbers=("NCHW", "OIHW", "NCHW"),
        preferred_element_type=jnp.float32,
    )
    return result[0]


def inflow(runoff_pad, dir_pad, extent_rows, extent_cols):
    inflow_sum = jnp.zeros((extent_rows, extent_cols), jnp.float32)
    for dir_code, (row_step, col_step) in enumerate(neighbour_steps):
        source_runoff = runoff_pad[
            1 - row_step : 1 - row_step + extent_rows, 1 - col_step : 1 - col_step + extent_cols
        ]
        source_dir = dir_pad[
            1 - row_step : 1 - row_step + extent_rows, 1 - col_step : 1 - col_step + extent_cols
        ]
        inflow_sum = inflow_sum + jnp.where(source_dir == dir_code, source_runoff, 0.0)
    return inflow_sum


def per_device(
    sar_image,
    kernel_first,
    kernel_second,
    kernel_third,
    kernel_last,
    geo_weight,
    cell_index,
    block_tile,
    block_row,
    depth,
    slope,
    flow_dir,
    rain,
):
    kernels = (kernel_first, kernel_second, kernel_third, kernel_last)
    devices = lax.axis_size(("tx", "ty"))
    az_lines = sar_image.shape[1]
    range_px = sar_image.shape[2]
    activation = sar_image
    logit = None
    for layer_no in range(4):
        padded = extended(activation, ((("tx", "ty"), 1),), 1)
        result = conv_rows(padded, kernels[layer_no])
        if layer_no < 3:
            activation = jnp.maximum(result, 0.0).astype(jnp.bfloat16)
        else:
            logit = result
    fraction = jax.nn.sigmoid(logit[0]).astype(jnp.bfloat16)
    tile_rows, tile_cols = depth.shape
    window_cells = WIN_ROWS * tile_cols
    weighted = fraction.astype(jnp.float32) * geo_weight
    line_block = math.gcd(az_lines, 32)
    block_count = az_lines // line_block
    window_cols = jnp.arange(window_cells, dtype=jnp.int32)

    def window_block(pieces):
        wet_blk, weight_blk, index_blk = pieces
        selector = (index_blk[:, :, None] == window_cols[None, None, :]).astype(jnp.float32)
        paired = jnp.stack([wet_blk, weight_blk], 1)
        return jnp.einsum(
            "lkp,lpc->lkc",
            paired,
            selector,
            precision=lax.Precision.HIGHEST,
            preferred_element_type=jnp.float32,
        )

    windows = lax.map(
        window_block,
        (
            weighted.reshape(block_count, line_block, range_px),
            geo_weight.reshape(block_count, line_block, range_px),
            cell_index.reshape(block_count, line_block, range_px),
        ),
    )
    windows = windows.reshape(az_lines, 2, window_cells)
    capacity = max(2, 2 * az_lines // devices)
    target_tile = block_tile[:, 0]
    onehot = (target_tile[:, None] == jnp.arange(devices, dtype=jnp.int32)[None, :]).astype(
        jnp.int32
    )
    earlier = jnp.sum((jnp.cumsum(onehot, 0) - onehot) * onehot, 1)
    slot_index = target_tile * capacity + earlier
    send_windows = (
        jnp.zeros((devices * capacity, 2, window_cells), jnp.float32).at[slot_index].set(windows)
    )
    send_rows = (
        jnp.zeros((devices * capacity,), jnp.float32)
        .at[slot_index]
        .set(block_row[:, 0].astype(jnp.float32))
    )
    got_windows, got_rows = (
        lax.all_to_all(
            send_windows.reshape(devices, capacity, 2, window_cells).astype(jnp.bfloat16),
            ("tx", "ty"),
            split_axis=0,
            concat_axis=0,
            tiled=True,
        ).astype(jnp.float32),
        lax.all_to_all(
            send_rows.reshape(devices, capacity).astype(jnp.bfloat16),
            ("tx", "ty"),
            split_axis=0,
            concat_axis=0,
            tiled=True,
        ).astype(jnp.float32),
    )
    slot_total = devices * capacity
    got_windows = got_windows.reshape(slot_total, 2, WIN_ROWS, tile_cols)
    got_lines = got_rows.reshape(-1).astype(jnp.int32)
    row_ids = jnp.arange(tile_rows, dtype=jnp.int32)
    offsets = jnp.arange(WIN_ROWS, dtype=jnp.int32)
    placer = (row_ids[None, :, None] == got_lines[None, None, :] + offsets[:, None, None]).astype(
        jnp.float32
    )
    summed = jnp.einsum(
        "wrs,skwc->krc",
        placer,
        got_windows,
        precision=lax.Precision.HIGHEST,
        preferred_element_type=jnp.float32,
    )
    observed = summed[0]
    covered = summed[1]
    wet = depth / (depth + wet_depth)
    innovation = (observed - covered * wet) / (covered + 1.0)
    level = depth * jnp.exp(innovation)
    conveyance = runoff_coef * jnp.sqrt(slope)
    dir_pad = extended(flow_dir, (("tx", 0), ("ty", 1)), 1)
    for substep in range(SUBSTEPS):
        runoff = conveyance * level * jnp.cbrt(level) * jnp.cbrt(level)
        runoff_pad = extended(runoff.astype(jnp.bfloat16), (("tx", 0), ("ty", 1)), 1).astype(
            runoff.dtype
        )
        level = level + rain - runoff + inflow(runoff_pad, dir_pad, tile_rows, tile_cols)
    return (fraction, level)


def solution(mesh):
    placed = (
        P(None, ("tx", "ty"), None),
        P(),
        P(),
        P(),
        P(),
        P(("tx", "ty"), None),
        P(("tx", "ty"), None),
        P(("tx", "ty"), None),
        P(("tx", "ty"), None),
        P("tx", "ty"),
        P("tx", "ty"),
        P("tx", "ty"),
        P("tx", "ty"),
    )
    return jax.shard_map(
        per_device,
        mesh=mesh,
        in_specs=placed,
        out_specs=(P(("tx", "ty"), None), P("tx", "ty")),
        check_vma=False,
    )
```

profile of v0, /device:TPU:7, one launch (start us, length us, event | category | flops | bytes accessed | tf_op | source)
XLA Modules:
  0.0 406.8 jit_solution(16226557317405317183)
XLA Ops:
  1.4 3.8 collective-permute-start
  13.2 6.0 %fusion.174 = bf16[2,66,8,67]{2,0,3,1:T(2,128)(2,1)S(1)} fusion(bf16[2,66,1,7,2]{3,0,4,1,2:T(2,128)(2,1)S(1)} %slice.544, bf16[2,66,1,8,65]{3,0,4,1,2:T(2,128)(2,1)S(1)} %copy.77), kind=kLoop, calls=%fused_computation.45.clone.clone.1 | loop fusion | flops 424512 | bytes 282480 | tf_op jit(solution)/shard_map/conv_general_dilated | solution.py:31
  19.2 13.8 %maximum_convert_fusion.2 = bf16[64,8,65,16]{3,1,2,0:T(8,128)(2,1)} fusion(bf16[16,2,3,3]{0,1,3,2:T(2,128)(2,1)} %param.16, pred[8,65]{0,1:T(8,128)(4,1)} %constant.75, bf16[2,66,8,67]{2,0,3,1:T(2,128)(2,1)S(1)} %fusion.174), kind=kOutput, calls=%fused_computation.23 | convolution fusion | flops 20766720 | bytes 1207560 | tf_op jit(solution)/shard_map/conv_general_dilated | solution.py:31
  33.0 8.2 %copy.78 = bf16[64,8,65,16]{2,1,3,0:T(8,128)(2,1)S(1)} copy(bf16[64,8,65,16]{3,1,2,0:T(8,128)(2,1)} %maximum_convert_fusion.2) | data formatting | bytes 2129920 | tf_op jit(solution)/shard_map/convert_element_type | solution.py:80
  53.4 8.1 %copy.80 = bf16[16,66,1,8,65]{0,3,4,1,2:T(8,128)(2,1)} copy(bf16[16,66,1,8,65]{4,3,0,1,2:T(8,128)(2,1)S(1)} %reshape.104) | data formatting | bytes 2196480 | tf_op jit(solution)/shard_map/conv_general_dilated | solution.py:31
  62.6 15.4 %maximum_convert_fusion.1 = bf16[64,8,65,16]{3,1,2,0:T(8,128)(2,1)} fusion(bf16[16,16,3,3]{1,0,3,2:T(8,128)(2,1)S(1)} %copy-done, bf16[16,66,1,7,2]{0,3,4,1,2:T(8,128)(2,1)S(1)} %slice.548, bf16[16,66,1,8,65]{0,3,4,1,2:T(8,128)(2,1)} %copy.80, pred[8,65]{0,1:T(8,128)(4,1)S(1)} %copy-done.16), kind=kOutput, calls=%fused_computation.22 | convolution fusion | flops 158347776 | bytes 2197896 | tf_op jit(solution)/shard_map/conv_general_dilated | solution.py:31
  78.0 8.2 %copy.81 = bf16[64,8,65,16]{2,1,3,0:T(8,128)(2,1)S(1)} copy(bf16[64,8,65,16]{3,1,2,0:T(8,128)(2,1)} %maximum_convert_fusion.1) | data formatting | bytes 2129920 | tf_op jit(solution)/shard_map/convert_element_type | solution.py:80
  90.0 5.2 %collective-permute-start.5 = (bf16[16,1,512]{2,0,1:T(8,128)(2,1)S(1)}, bf16[16,1,512]{2,0,1:T(8,128)(2,1)S(1)}, u32[]{:S(2)}, u32[]{:S(2)}) collective-permute-start(bf16[16,1,512]{2,0,1:T(8,128)(2,1)S(1)} %get-tuple-element.113), channel_id=1, source_target_pairs={{1,0},{2,1},{3,2},{4,3},{5,4},{6,5},{7,6},{8,7},{9,8},{10,9},{11,1... | collective-permute-start | bytes 49160 | tf_op jit(solution)/shard_map/ppermute | solution.py:25
  98.5 8.1 %copy.83 = bf16[16,66,1,8,65]{0,3,4,1,2:T(8,128)(2,1)} copy(bf16[16,66,1,8,65]{4,3,0,1,2:T(8,128)(2,1)S(1)} %reshape.111) | data formatting | bytes 2196480 | tf_op jit(solution)/shard_map/conv_general_dilated | solution.py:31
  107.7 15.4 %maximum_convert_fusion = bf16[64,8,65,16]{3,1,2,0:T(8,128)(2,1)} fusion(bf16[16,16,3,3]{1,0,3,2:T(8,128)(2,1)} %param.18, bf16[16,66,1,7,2]{0,3,4,1,2:T(8,128)(2,1)S(1)} %slice.552, bf16[16,66,1,8,65]{0,3,4,1,2:T(8,128)(2,1)} %copy.83, pred[8,65]{0,1:T(8,128)(4,1)S(1)} %copy-done.17), kind=kOutput, calls=%fused_computation.21 | convolution fusion | flops 158347776 | bytes 2197896 | tf_op jit(solution)/shard_map/conv_general_dilated | solution.py:31
  123.1 8.2 %copy.84 = bf16[64,8,65,16]{2,1,3,0:T(8,128)(2,1)S(1)} copy(bf16[64,8,65,16]{3,1,2,0:T(8,128)(2,1)} %maximum_convert_fusion) | data formatting | bytes 2129920 | tf_op jit(solution)/shard_map/convert_element_type | solution.py:80
  135.1 6.4 %collective-permute-start.7 = (bf16[16,1,512]{2,0,1:T(8,128)(2,1)S(1)}, bf16[16,1,512]{2,0,1:T(8,128)(2,1)S(1)}, u32[]{:S(2)}, u32[]{:S(2)}) collective-permute-start(bf16[16,1,512]{2,0,1:T(8,128)(2,1)S(1)} %get-tuple-element.111), channel_id=1, source_target_pairs={{1,0},{2,1},{3,2},{4,3},{5,4},{6,5},{7,6},{8,7},{9,8},{10,9},{11,1... | collective-permute-start | bytes 49160 | tf_op jit(solution)/shard_map/ppermute | solution.py:25
  143.1 18.1 %all-to-all-start.1 = ((bf16[128,1,2]{2,1,0:T(2,128)(2,1)}), bf16[128,1,2]{2,1,0:T(2,128)(2,1)}, u32[]{:S(2)}, u32[]{:S(2)}) async-start(bf16[128,1,2]{2,1,0:T(2,128)(2,1)} %convert_element_type.153), calls=%async_computation.1 | async-start | bytes 131072 | tf_op jit(solution)/shard_map/all_to_all | solution.py:135
  164.3 8.2 %copy.86 = bf16[16,66,1,8,65]{0,3,4,1,2:T(8,128)(2,1)} copy(bf16[16,66,1,8,65]{4,3,0,1,2:T(8,128)(2,1)S(1)} %reshape.118) | data formatting | bytes 2196480 | tf_op jit(solution)/shard_map/conv_general_dilated | solution.py:31
  173.5 15.5 %fusion.21 = f32[64,8,65,1]{3,1,2,0:T(8,128)} fusion(bf16[16,66,1,7,2]{0,3,4,1,2:T(8,128)(2,1)S(1)} %slice.556, bf16[16,66,1,8,65]{0,3,4,1,2:T(8,128)(2,1)} %copy.86, bf16[1,16,3,3]{1,3,2,0:T(4,128)(2,1)S(1)} %copy-done.15), kind=kOutput, calls=%fused_computation.30 | convolution fusion | flops 12980736 | bytes 1261216 | tf_op jit(solution)/shard_map/conv_general_dilated | solution.py:31
  189.0 10.1 %copy.88 = f32[64,8,65,1]{2,1,3,0:T(8,128)S(1)} copy(f32[64,8,65,1]{3,1,2,0:T(8,128)} %fusion.21) | data formatting | bytes 266240 | tf_op jit(solution)/shard_map/conv_general_dilated | solution.py:31
  200.1 26.8 %while.11 = (s32[]{:T(128)}, f32[2,32,2,512]{3,2,1,0:T(2,128)S(1)}, f32[2,32,512]{2,1,0:T(8,128)S(1)}, f32[2,32,512]{2,1,0:T(8,128)S(1)}, s32[2,32,512]{2,1,0:T(8,128)S(1)}, /*index=5*/s32[]{:T(128)}) while((s32[]{:T(128)}, f32[2,32,2,512]{3,2,1,0:T(2,128)S(1)}, f32[2,32,512]{2,1,0:T(8,128)S(1)}, f32[2,32,512]{2,1,0:T(8,128)S(1)}, ...), condition=%wide.region_3.4_spmd.clone, body=%wide.region_2.3_spmd.clone.sunk | while | flops 209747968 | bytes 983121 | solution.py:103
  200.3 13.2 %fusion.179 = f32[2,32,2,512]{3,2,1,0:T(2,128)S(1)} fusion(f32[2,32,2,512]{3,2,1,0:T(2,128)S(1)} %get-tuple-element.200, s32[]{:T(128)} %get-tuple-element.199, s32[32,512]{1,0:T(8,128)S(1)} %dynamic-slice_bitcast_fusion.2, f32[32,1,512]{2,1,0:T(1,128)S(1)} %bitcast.127, f32[32,1,512]{2,1,0:T(1,128)S(1)} %bitcast.128), kind=kOutput, calls=%fused_computation.7.clone.1 | convolution fusion | flops 209747968 | bytes 327684 | tf_op jit(solution)/shard_map/while/body/eval_jaxpr/lkp,lpc->lkc/dot_general | solution.py:95
  213.7 13.2 %fusion.179 = f32[2,32,2,512]{3,2,1,0:T(2,128)S(1)} fusion(f32[2,32,2,512]{3,2,1,0:T(2,128)S(1)} %get-tuple-element.200, s32[]{:T(128)} %get-tuple-element.199, s32[32,512]{1,0:T(8,128)S(1)} %dynamic-slice_bitcast_fusion.2, f32[32,1,512]{2,1,0:T(1,128)S(1)} %bitcast.127, f32[32,1,512]{2,1,0:T(1,128)S(1)} %bitcast.128), kind=kOutput, calls=%fused_computation.7.clone.1 | convolution fusion | flops 209747968 | bytes 327684 | tf_op jit(solution)/shard_map/while/body/eval_jaxpr/lkp,lpc->lkc/dot_general | solution.py:95
  230.8 9.8 %all-to-all-start = ((bf16[128,2,2,512]{3,2,1,0:T(2,128)(2,1)}), bf16[128,2,2,512]{3,2,1,0:T(2,128)(2,1)S(1)}, u32[]{:S(2)}, u32[]{:S(2)}) async-start(bf16[128,2,2,512]{3,2,1,0:T(2,128)(2,1)} %bitcast.25), calls=%async_computation | async-start | bytes 1048576 | tf_op jit(solution)/shard_map/all_to_all | solution.py:128
  247.1 3.4 collective-permute-done.9
  253.5 3.7 collective-permute-start.11
  259.2 3.5 collective-permute-start.10
  274.2 5.5 %collective-permute-start.16 = (bf16[1,256]{1,0:T(2,128)(2,1)S(1)}, bf16[1,256]{1,0:T(2,128)(2,1)S(1)}, u32[]{:S(2)}, u32[]{:S(2)}) collective-permute-start(bf16[1,256]{1,0:T(2,128)(2,1)S(1)} %get-tuple-element.150), channel_id=1, source_target_pairs={{0,8},{8,16},{16,24},{24,32},{32,40},{40,48},{48,56},{56,64},{64,7... | collective-permute-start | bytes 1544 | tf_op jit(solution)/shard_map/ppermute | solution.py:24
  281.6 4.5 %collective-permute-done.17 = bf16[1,256]{1,0:T(2,128)(2,1)S(1)} collective-permute-done((bf16[1,256]{1,0:T(2,128)(2,1)S(1)}, bf16[1,256]{1,0:T(2,128)(2,1)S(1)}, u32[]{:S(2)}, u32[]{:S(2)}) %collective-permute-start.17) | collective-permute-done | bytes 544 | tf_op jit(solution)/shard_map/ppermute | solution.py:25
  291.4 3.7 collective-permute-done.19
  309.7 3.7 collective-permute-done.23
  328.0 3.7 collective-permute-done.27
  346.3 3.7 collective-permute-done.31
  364.6 3.7 collective-permute-done.35
  382.9 3.7 collective-permute-done.39
  401.2 3.7 collective-permute-done.43
  (210 shorter events, 163.5 us)
Async XLA Ops:
  1.4 5.7 %collective-permute-start = (bf16[2,1,512]{2,1,0:T(2,128)(2,1)S(1)}, bf16[2,1,512]{2,1,0:T(2,128)(2,1)S(1)}, u32[]{:S(2)}, u32[]{:S(2)}) collective-permute-start(bf16[2,1,512]{2,1,0:T(2,128)(2,1)S(1)} %get-tuple-element.154), channel_id=1, source_target_pairs={{0,1},{1,2},{2,3},{3,4},{4,5},{5,6},{6,7},{7,8},{8,9},{9,10},{10,1... | collective-permute-start | bytes 6152 | tf_op jit(solution)/shard_map/ppermute | solution.py:24
  43.0 5.9 %collective-permute-start.2 = (bf16[16,1,512]{2,0,1:T(8,128)(2,1)S(1)}, bf16[16,1,512]{2,0,1:T(8,128)(2,1)S(1)}, u32[]{:S(2)}, u32[]{:S(2)}) collective-permute-start(bf16[16,1,512]{2,0,1:T(8,128)(2,1)S(1)} %get-tuple-element.114), channel_id=1, source_target_pairs={{0,1},{1,2},{2,3},{3,4},{4,5},{5,6},{6,7},{7,8},{8,9},{9,10},{10,1... | collective-permute-start | bytes 49160 | tf_op jit(solution)/shard_map/ppermute | solution.py:24
  45.0 5.4 %collective-permute-start.3 = (bf16[16,1,512]{2,0,1:T(8,128)(2,1)S(1)}, bf16[16,1,512]{2,0,1:T(8,128)(2,1)S(1)}, u32[]{:S(2)}, u32[]{:S(2)}) collective-permute-start(bf16[16,1,512]{2,0,1:T(8,128)(2,1)S(1)} %get-tuple-element.115), channel_id=1, source_target_pairs={{1,0},{2,1},{3,2},{4,3},{5,4},{6,5},{7,6},{8,7},{9,8},{10,9},{11,1... | collective-permute-start | bytes 49160 | tf_op jit(solution)/shard_map/ppermute | solution.py:25
  88.0 7.3 %collective-permute-start.4 = (bf16[16,1,512]{2,0,1:T(8,128)(2,1)S(1)}, bf16[16,1,512]{2,0,1:T(8,128)(2,1)S(1)}, u32[]{:S(2)}, u32[]{:S(2)}) collective-permute-start(bf16[16,1,512]{2,0,1:T(8,128)(2,1)S(1)} %get-tuple-element.112), channel_id=1, source_target_pairs={{0,1},{1,2},{2,3},{3,4},{4,5},{5,6},{6,7},{7,8},{8,9},{9,10},{10,1... | collective-permute-start | bytes 49160 | tf_op jit(solution)/shard_map/ppermute | solution.py:24
  90.0 5.5 %collective-permute-start.5 = (bf16[16,1,512]{2,0,1:T(8,128)(2,1)S(1)}, bf16[16,1,512]{2,0,1:T(8,128)(2,1)S(1)}, u32[]{:S(2)}, u32[]{:S(2)}) collective-permute-start(bf16[16,1,512]{2,0,1:T(8,128)(2,1)S(1)} %get-tuple-element.113), channel_id=1, source_target_pairs={{1,0},{2,1},{3,2},{4,3},{5,4},{6,5},{7,6},{8,7},{9,8},{10,9},{11,1... | collective-permute-start | bytes 49160 | tf_op jit(solution)/shard_map/ppermute | solution.py:25
  133.2 28.0 %collective-permute-start.6 = (bf16[16,1,512]{2,0,1:T(8,128)(2,1)S(1)}, bf16[16,1,512]{2,0,1:T(8,128)(2,1)S(1)}, u32[]{:S(2)}, u32[]{:S(2)}) collective-permute-start(bf16[16,1,512]{2,0,1:T(8,128)(2,1)S(1)} %get-tuple-element.110), channel_id=1, source_target_pairs={{0,1},{1,2},{2,3},{3,4},{4,5},{5,6},{6,7},{7,8},{8,9},{9,10},{10,1... | collective-permute-start | bytes 49160 | tf_op jit(solution)/shard_map/ppermute | solution.py:24
  135.1 26.1 %collective-permute-start.7 = (bf16[16,1,512]{2,0,1:T(8,128)(2,1)S(1)}, bf16[16,1,512]{2,0,1:T(8,128)(2,1)S(1)}, u32[]{:S(2)}, u32[]{:S(2)}) collective-permute-start(bf16[16,1,512]{2,0,1:T(8,128)(2,1)S(1)} %get-tuple-element.111), channel_id=1, source_target_pairs={{1,0},{2,1},{3,2},{4,3},{5,4},{6,5},{7,6},{8,7},{9,8},{10,9},{11,1... | collective-permute-start | bytes 49160 | tf_op jit(solution)/shard_map/ppermute | solution.py:25
  143.1 87.7 %all-to-all-start.1 = ((bf16[128,1,2]{2,1,0:T(2,128)(2,1)}), bf16[128,1,2]{2,1,0:T(2,128)(2,1)}, u32[]{:S(2)}, u32[]{:S(2)}) async-start(bf16[128,1,2]{2,1,0:T(2,128)(2,1)} %convert_element_type.153), calls=%async_computation.1 | async-start | bytes 131072 | tf_op jit(solution)/shard_map/all_to_all | solution.py:135
  230.8 21.6 %all-to-all-start = ((bf16[128,2,2,512]{3,2,1,0:T(2,128)(2,1)}), bf16[128,2,2,512]{3,2,1,0:T(2,128)(2,1)S(1)}, u32[]{:S(2)}, u32[]{:S(2)}) async-start(bf16[128,2,2,512]{3,2,1,0:T(2,128)(2,1)} %bitcast.25), calls=%async_computation | async-start | bytes 1048576 | tf_op jit(solution)/shard_map/all_to_all | solution.py:128
  240.6 6.5 %collective-permute-start.8 = (s32[1,256]{1,0:T(1,128)S(1)}, s32[1,256]{1,0:T(1,128)S(1)}, u32[]{:S(2)}, u32[]{:S(2)}) collective-permute-start(s32[1,256]{1,0:T(1,128)S(1)} %get-tuple-element.120), channel_id=1, source_target_pairs={{0,8},{8,16},{16,24},{24,32},{32,40},{40,48},{48,56},{56,64},{64,7... | collective-permute-start | bytes 3080 | tf_op jit(solution)/shard_map/ppermute | solution.py:24
  243.8 6.7 %collective-permute-start.9 = (s32[1,256]{1,0:T(1,128)S(1)}, s32[1,256]{1,0:T(1,128)S(1)}, u32[]{:S(2)}, u32[]{:S(2)}) collective-permute-start(s32[1,256]{1,0:T(1,128)S(1)} %get-tuple-element.121), channel_id=1, source_target_pairs={{8,0},{16,8},{24,16},{32,24},{40,32},{48,40},{56,48},{64,56},{72,6... | collective-permute-start | bytes 3080 | tf_op jit(solution)/shard_map/ppermute | solution.py:25
  253.5 11.4 %collective-permute-start.11 = (bf16[1,256]{1,0:T(2,128)(2,1)S(1)}, bf16[1,256]{1,0:T(2,128)(2,1)S(1)}, u32[]{:S(2)}, u32[]{:S(2)}) collective-permute-start(bf16[1,256]{1,0:T(2,128)(2,1)S(1)} %get-tuple-element.152), channel_id=1, source_target_pairs={{0,8},{8,16},{16,24},{24,32},{32,40},{40,48},{48,56},{56,64},{64,7... | collective-permute-start | bytes 1544 | tf_op jit(solution)/shard_map/ppermute | solution.py:24
  257.2 7.6 %collective-permute-start.12 = (bf16[1,256]{1,0:T(2,128)(2,1)S(1)}, bf16[1,256]{1,0:T(2,128)(2,1)S(1)}, u32[]{:S(2)}, u32[]{:S(2)}) collective-permute-start(bf16[1,256]{1,0:T(2,128)(2,1)S(1)} %get-tuple-element.153), channel_id=1, source_target_pairs={{8,0},{16,8},{24,16},{32,24},{40,32},{48,40},{56,48},{64,56},{72,6... | collective-permute-start | bytes 1544 | tf_op jit(solution)/shard_map/ppermute | solution.py:25
  259.2 10.7 %collective-permute-start.10 = (s32[258,1]{1,0:T(8,128)S(1)}, s32[258,1]{1,0:T(8,128)S(1)}, u32[]{:S(2)}, u32[]{:S(2)}) collective-permute-start(s32[258,1]{1,0:T(8,128)S(1)} %get-tuple-element.117), channel_id=1, source_target_pairs={{1,0},{2,1},{3,2},{4,3},{5,4},{6,5},{7,6},{9,8},{10,9},{11,10},{12... | collective-permute-start | bytes 3104 | tf_op jit(solution)/shard_map/ppermute | solution.py:25
  262.7 7.2 %collective-permute-start.15 = (s32[258,1]{1,0:T(8,128)S(1)}, s32[258,1]{1,0:T(8,128)S(1)}, u32[]{:S(2)}, u32[]{:S(2)}) collective-permute-start(s32[258,1]{1,0:T(8,128)S(1)} %get-tuple-element.116), channel_id=1, source_target_pairs={{0,1},{1,2},{2,3},{3,4},{4,5},{5,6},{6,7},{8,9},{9,10},{10,11},{11... | collective-permute-start | bytes 3104 | tf_op jit(solution)/shard_map/ppermute | solution.py:24
  267.1 5.6 %collective-permute-start.14 = (bf16[258,1]{1,0:T(8,128)(2,1)S(1)}, bf16[258,1]{1,0:T(8,128)(2,1)S(1)}, u32[]{:S(2)}, u32[]{:S(2)}) collective-permute-start(bf16[258,1]{1,0:T(8,128)(2,1)S(1)} %get-tuple-element.137), channel_id=1, source_target_pairs={{1,0},{2,1},{3,2},{4,3},{5,4},{6,5},{7,6},{9,8},{10,9},{11,10},{12... | collective-permute-start | bytes 1556 | tf_op jit(solution)/shard_map/ppermute | solution.py:25
  274.2 7.4 %collective-permute-start.16 = (bf16[1,256]{1,0:T(2,128)(2,1)S(1)}, bf16[1,256]{1,0:T(2,128)(2,1)S(1)}, u32[]{:S(2)}, u32[]{:S(2)}) collective-permute-start(bf16[1,256]{1,0:T(2,128)(2,1)S(1)} %get-tuple-element.150), channel_id=1, source_target_pairs={{0,8},{8,16},{16,24},{24,32},{32,40},{40,48},{48,56},{56,64},{64,7... | collective-permute-start | bytes 1544 | tf_op jit(solution)/shard_map/ppermute | solution.py:24
  279.6 6.4 %collective-permute-start.17 = (bf16[1,256]{1,0:T(2,128)(2,1)S(1)}, bf16[1,256]{1,0:T(2,128)(2,1)S(1)}, u32[]{:S(2)}, u32[]{:S(2)}) collective-permute-start(bf16[1,256]{1,0:T(2,128)(2,1)S(1)} %get-tuple-element.151), channel_id=1, source_target_pairs={{8,0},{16,8},{24,16},{32,24},{40,32},{48,40},{56,48},{64,56},{72,6... | collective-permute-start | bytes 1544 | tf_op jit(solution)/shard_map/ppermute | solution.py:25
  289.5 5.6 %collective-permute-start.19 = (bf16[258,1]{1,0:T(8,128)(2,1)S(1)}, bf16[258,1]{1,0:T(8,128)(2,1)S(1)}, u32[]{:S(2)}, u32[]{:S(2)}) collective-permute-start(bf16[258,1]{1,0:T(8,128)(2,1)S(1)} %get-tuple-element.135), channel_id=1, source_target_pairs={{1,0},{2,1},{3,2},{4,3},{5,4},{6,5},{7,6},{9,8},{10,9},{11,10},{12... | collective-permute-start | bytes 1556 | tf_op jit(solution)/shard_map/ppermute | solution.py:25
  296.3 5.3 %collective-permute-start.20 = (bf16[1,256]{1,0:T(2,128)(2,1)S(1)}, bf16[1,256]{1,0:T(2,128)(2,1)S(1)}, u32[]{:S(2)}, u32[]{:S(2)}) collective-permute-start(bf16[1,256]{1,0:T(2,128)(2,1)S(1)} %get-tuple-element.148), channel_id=1, source_target_pairs={{0,8},{8,16},{16,24},{24,32},{32,40},{40,48},{48,56},{56,64},{64,7... | collective-permute-start | bytes 1544 | tf_op jit(solution)/shard_map/ppermute | solution.py:24
  298.2 6.4 %collective-permute-start.21 = (bf16[1,256]{1,0:T(2,128)(2,1)S(1)}, bf16[1,256]{1,0:T(2,128)(2,1)S(1)}, u32[]{:S(2)}, u32[]{:S(2)}) collective-permute-start(bf16[1,256]{1,0:T(2,128)(2,1)S(1)} %get-tuple-element.149), channel_id=1, source_target_pairs={{8,0},{16,8},{24,16},{32,24},{40,32},{48,40},{56,48},{64,56},{72,6... | collective-permute-start | bytes 1544 | tf_op jit(solution)/shard_map/ppermute | solution.py:25
  307.8 5.6 %collective-permute-start.23 = (bf16[258,1]{1,0:T(8,128)(2,1)S(1)}, bf16[258,1]{1,0:T(8,128)(2,1)S(1)}, u32[]{:S(2)}, u32[]{:S(2)}) collective-permute-start(bf16[258,1]{1,0:T(8,128)(2,1)S(1)} %get-tuple-element.133), channel_id=1, source_target_pairs={{1,0},{2,1},{3,2},{4,3},{5,4},{6,5},{7,6},{9,8},{10,9},{11,10},{12... | collective-permute-start | bytes 1556 | tf_op jit(solution)/shard_map/ppermute | solution.py:25
  316.5 6.4 %collective-permute-start.25 = (bf16[1,256]{1,0:T(2,128)(2,1)S(1)}, bf16[1,256]{1,0:T(2,128)(2,1)S(1)}, u32[]{:S(2)}, u32[]{:S(2)}) collective-permute-start(bf16[1,256]{1,0:T(2,128)(2,1)S(1)} %get-tuple-element.147), channel_id=1, source_target_pairs={{8,0},{16,8},{24,16},{32,24},{40,32},{48,40},{56,48},{64,56},{72,6... | collective-permute-start | bytes 1544 | tf_op jit(solution)/shard_map/ppermute | solution.py:25
  326.1 5.6 %collective-permute-start.27 = (bf16[258,1]{1,0:T(8,128)(2,1)S(1)}, bf16[258,1]{1,0:T(8,128)(2,1)S(1)}, u32[]{:S(2)}, u32[]{:S(2)}) collective-permute-start(bf16[258,1]{1,0:T(8,128)(2,1)S(1)} %get-tuple-element.131), channel_id=1, source_target_pairs={{1,0},{2,1},{3,2},{4,3},{5,4},{6,5},{7,6},{9,8},{10,9},{11,10},{12... | collective-permute-start | bytes 1556 | tf_op jit(solution)/shard_map/ppermute | solution.py:25
  334.8 6.4 %collective-permute-start.29 = (bf16[1,256]{1,0:T(2,128)(2,1)S(1)}, bf16[1,256]{1,0:T(2,128)(2,1)S(1)}, u32[]{:S(2)}, u32[]{:S(2)}) collective-permute-start(bf16[1,256]{1,0:T(2,128)(2,1)S(1)} %get-tuple-element.145), channel_id=1, source_target_pairs={{8,0},{16,8},{24,16},{32,24},{40,32},{48,40},{56,48},{64,56},{72,6... | collective-permute-start | bytes 1544 | tf_op jit(solution)/shard_map/ppermute | solution.py:25
  344.4 5.6 %collective-permute-start.31 = (bf16[258,1]{1,0:T(8,128)(2,1)S(1)}, bf16[258,1]{1,0:T(8,128)(2,1)S(1)}, u32[]{:S(2)}, u32[]{:S(2)}) collective-permute-start(bf16[258,1]{1,0:T(8,128)(2,1)S(1)} %get-tuple-element.129), channel_id=1, source_target_pairs={{1,0},{2,1},{3,2},{4,3},{5,4},{6,5},{7,6},{9,8},{10,9},{11,10},{12... | collective-permute-start | bytes 1556 | tf_op jit(solution)/shard_map/ppermute | solution.py:25
  353.1 6.4 %collective-permute-start.33 = (bf16[1,256]{1,0:T(2,128)(2,1)S(1)}, bf16[1,256]{1,0:T(2,128)(2,1)S(1)}, u32[]{:S(2)}, u32[]{:S(2)}) collective-permute-start(bf16[1,256]{1,0:T(2,128)(2,1)S(1)} %get-tuple-element.143), channel_id=1, source_target_pairs={{8,0},{16,8},{24,16},{32,24},{40,32},{48,40},{56,48},{64,56},{72,6... | collective-permute-start | bytes 1544 | tf_op jit(solution)/shard_map/ppermute | solution.py:25
  362.7 5.6 %collective-permute-start.35 = (bf16[258,1]{1,0:T(8,128)(2,1)S(1)}, bf16[258,1]{1,0:T(8,128)(2,1)S(1)}, u32[]{:S(2)}, u32[]{:S(2)}) collective-permute-start(bf16[258,1]{1,0:T(8,128)(2,1)S(1)} %get-tuple-element.127), channel_id=1, source_target_pairs={{1,0},{2,1},{3,2},{4,3},{5,4},{6,5},{7,6},{9,8},{10,9},{11,10},{12... | collective-permute-start | bytes 1556 | tf_op jit(solution)/shard_map/ppermute | solution.py:25
  371.4 6.4 %collective-permute-start.37 = (bf16[1,256]{1,0:T(2,128)(2,1)S(1)}, bf16[1,256]{1,0:T(2,128)(2,1)S(1)}, u32[]{:S(2)}, u32[]{:S(2)}) collective-permute-start(bf16[1,256]{1,0:T(2,128)(2,1)S(1)} %get-tuple-element.141), channel_id=1, source_target_pairs={{8,0},{16,8},{24,16},{32,24},{40,32},{48,40},{56,48},{64,56},{72,6... | collective-permute-start | bytes 1544 | tf_op jit(solution)/shard_map/ppermute | solution.py:25
  381.0 5.6 %collective-permute-start.39 = (bf16[258,1]{1,0:T(8,128)(2,1)S(1)}, bf16[258,1]{1,0:T(8,128)(2,1)S(1)}, u32[]{:S(2)}, u32[]{:S(2)}) collective-permute-start(bf16[258,1]{1,0:T(8,128)(2,1)S(1)} %get-tuple-element.125), channel_id=1, source_target_pairs={{1,0},{2,1},{3,2},{4,3},{5,4},{6,5},{7,6},{9,8},{10,9},{11,10},{12... | collective-permute-start | bytes 1556 | tf_op jit(solution)/shard_map/ppermute | solution.py:25
  389.7 6.4 %collective-permute-start.41 = (bf16[1,256]{1,0:T(2,128)(2,1)S(1)}, bf16[1,256]{1,0:T(2,128)(2,1)S(1)}, u32[]{:S(2)}, u32[]{:S(2)}) collective-permute-start(bf16[1,256]{1,0:T(2,128)(2,1)S(1)} %get-tuple-element.139), channel_id=1, source_target_pairs={{8,0},{16,8},{24,16},{32,24},{40,32},{48,40},{56,48},{64,56},{72,6... | collective-permute-start | bytes 1544 | tf_op jit(solution)/shard_map/ppermute | solution.py:25
  399.3 5.6 %collective-permute-start.43 = (bf16[258,1]{1,0:T(8,128)(2,1)S(1)}, bf16[258,1]{1,0:T(8,128)(2,1)S(1)}, u32[]{:S(2)}, u32[]{:S(2)}) collective-permute-start(bf16[258,1]{1,0:T(8,128)(2,1)S(1)} %get-tuple-element.123), channel_id=1, source_target_pairs={{1,0},{2,1},{3,2},{4,3},{5,4},{6,5},{7,6},{9,8},{10,9},{11,10},{12... | collective-permute-start | bytes 1556 | tf_op jit(solution)/shard_map/ppermute | solution.py:25
  (32 other events, 555.8 us)
where the time goes:
time: 414 us; the launch traced here: 407 us
  starting transfers between devices  149 us (36%)
  matrix products  86.8 us (21%)
  local copies, waits for them, and re-layouts  85.4 us (21%)
  waiting for transfers between devices  60.8 us (15%)
  other arithmetic  22.2 us (5%)
    ppermute x22, starting transfers between devices, extended(): after = lax.ppermute(leading, axis, down)  62.5 us
    conv_general_dilated x4, matrix products, conv_rows(): lax.conv_general_dilated(activation[None], kernel, (1, 1), ((0, 0), (1, 1...  60.1 us
    ppermute x22, starting transfers between devices, extended(): before = lax.ppermute(last, axis, up)  59 us
    ppermute x22, waiting for transfers between devices, extended(): after = lax.ppermute(leading, axis, down)  58.9 us
    conv_general_dilated x13, local copies, waits for them, and re-layouts, conv_rows(): lax.conv_general_dilated(activation[None], kernel, (1, 1), ((0, 0), (1, 1...  46.3 us
    convert_element_type x9, local copies, waits for them, and re-layouts, per_device(): activation = jnp.maximum(result, 0.0).astype(jnp.bfloat16)  30 us
    dot_general x2, matrix products, window_block(): jnp.einsum('lkp,lpc->lkc', paired, selector, precision=lax.Precision.HIGH...  26.4 us
    all_to_all x1, starting transfers between devices, per_device(): lax.all_to_all(send_rows.reshape(devices, capacity).astype(jnp.bfloat16),...  18.1 us
  transfers between devices with their start and end apart: 46, of which 20 were waited for; matrix products, arithmetic and copies ran while one was open for 18% of the time, Pallas kernels for 0%

commit v1 on v0

v1 whole, which is shorter than its diff:
```python
import functools

import jax
import jax.numpy as jnp
from jax import lax
from jax.experimental import pallas as pl
from jax.experimental.pallas import tpu as pltpu
from jax.sharding import PartitionSpec as P

F32 = jnp.float32
BF16 = jnp.bfloat16
I32 = jnp.int32

WIN_ROWS = 2
SUBSTEPS = 8
CAPACITY = 2
CHANNELS = 16
WET_DEPTH = 0.5
RUNOFF_COEF = 0.25

AZ = 64
PX = 512
HALO = 4
IMG_ROWS = 96
ROWS1 = 80
TILE = 256
DEPTH = 8
EXT_ROWS = TILE + 2 * DEPTH
EXT_COLS = TILE + 128

NN = (((1,), (0,)), ((), ()))
NT = (((1,), (1,)), ((), ()))
TN = (((0,), (0,)), ((), ()))


def dot(a, b, dims=NN):
    return lax.dot_general(a, b, dims, preferred_element_type=F32)


def iota(shape, dim):
    return lax.broadcasted_iota(I32, shape, dim)


def onehot(cond):
    return jnp.where(cond, 1.0, 0.0).astype(BF16)


def shifted(x, step):
    width = x.shape[1]
    rolled = pltpu.roll(x, step % width, 1)
    edge = 0 if step == 1 else width - 1
    return jnp.where(iota(x.shape, 1) == edge, 0.0, rolled)


def build_weights(ksmall_ref, k2_ref, k3_ref, w1_ref, w2_ref, w3_ref, w4_ref):
    spread = onehot(iota((16, 256), 1) % 16 == iota((16, 256), 0))
    band = iota((16, 256), 1) // 16
    for k_ref, w_ref in ((k2_ref, w2_ref), (k3_ref, w3_ref)):
        tiled = dot(k_ref[...], spread)
        for dx in range(3):
            taps = [tiled[(dy * 3 + dx) * 16 : (dy * 3 + dx + 1) * 16] for dy in range(3)]
            for row in range(14):
                value = jnp.zeros((16, 256), F32)
                for dy in range(3):
                    value = jnp.where(band == row + dy, taps[dy], value)
                w_ref[dx, row * 16 : (row + 1) * 16, :] = value.astype(BF16)
    lane = iota((32, 192), 1)
    taps = []
    for dy in range(3):
        source = (dy * 3 + lane // 64) * 2 + (lane // 32) % 2
        taps.append(dot(ksmall_ref[...], onehot(iota((32, 192), 0) == source), TN))
    in_row = iota((16, 192), 1) % 32
    for row in range(16):
        value = jnp.zeros((16, 192), F32)
        for dy in range(3):
            value = jnp.where(in_row == row + dy, taps[dy], value)
        w1_ref[row * 16 : (row + 1) * 16, :] = value.astype(BF16)
    tiled = dot(ksmall_ref[...], spread)
    band = iota((8, 256), 1) // 16 - iota((8, 256), 0)
    for dx in range(3):
        value = jnp.zeros((8, 256), F32)
        for dy in range(3):
            at = 18 + dy * 3 + dx
            value = jnp.where(band == dy, tiled[at : at + 1], value)
        w4_ref[dx * 8 : (dx + 1) * 8, :] = value


def put_rows(h_ref, at, value):
    rows = value.shape[0]
    h_ref[1, pl.ds(at, rows), :] = value.astype(BF16)
    h_ref[0, pl.ds(at, rows), :] = shifted(value, 1).astype(BF16)
    h_ref[2, pl.ds(at, rows), :] = shifted(value, -1).astype(BF16)


def clear_rows(h_ref, first, last, rows, width):
    for cond, start in ((first, 0), (last, rows - width)):

        @pl.when(cond)
        def _():
            h_ref[:, start * 16 : (start + width) * 16, :] = jnp.zeros((3, width * 16, PX), BF16)


def conv_layers(x_ref, xs_ref, w1_ref, w2_ref, w3_ref, w4_ref, ha_ref, hb_ref, first, last):
    for pol in range(2):
        value = x_ref[pol].astype(F32)
        base = pol * IMG_ROWS
        xs_ref[1, base : base + IMG_ROWS, :] = value.astype(BF16)
        xs_ref[0, base : base + IMG_ROWS, :] = shifted(value, 1).astype(BF16)
        xs_ref[2, base : base + IMG_ROWS, :] = shifted(value, -1).astype(BF16)
    for block in range(5):
        pieces = []
        for dx in range(3):
            for pol in range(2):
                at = pol * IMG_ROWS + block * 16
                pieces.append(xs_ref[dx, at : at + 32, :])
        value = dot(w1_ref[...], jnp.concatenate(pieces, 0))
        put_rows(ha_ref, block * 256, jnp.maximum(value, 0.0))
    clear_rows(ha_ref, first, last, 70, 3)
    hb_ref[:, 70 * 16 : 72 * 16, :] = jnp.zeros((3, 32, PX), BF16)
    for w_ref, src, dst, rows, width in (
        (w2_ref, ha_ref, hb_ref, 68, 2),
        (w3_ref, hb_ref, ha_ref, 66, 1),
    ):

        def block_body(block, carry):
            at = pl.multiple_of(block * 224, 32)
            value = dot(w_ref[0], src[0, pl.ds(at, 256), :])
            value = value + dot(w_ref[1], src[1, pl.ds(at, 256), :])
            value = value + dot(w_ref[2], src[2, pl.ds(at, 256), :])
            put_rows(dst, at, jnp.maximum(value, 0.0))
            return carry

        lax.fori_loop(0, 5, block_body, 0)
        clear_rows(dst, first, last, rows, width)


def last_layer(w4_ref, h_ref, logit_ref):
    for block in range(8):
        at = block * 128
        value = jnp.zeros((8, PX), F32)
        for dx in range(3):
            tap = w4_ref[dx * 8 : (dx + 1) * 8, 0:160].astype(BF16)
            value = value + dot(tap, h_ref[dx, at : at + 160, :])
        logit_ref[block * 8 : (block + 1) * 8, :] = value


def line_sums(value_ref, cell_ref, win_ref):
    cells = iota((128, PX), 0)
    quarter = iota((8, PX), 0)

    def pair(step, carry):
        parts, picks = [], []
        for k in range(2):
            line = step * 2 + k
            cell = cell_ref[pl.ds(line, 1), :]
            value = value_ref[pl.ds(line, 1), :]
            high = value.astype(BF16).astype(F32)
            picks.append(onehot(cells == cell % 128))
            here = quarter == cell // 128 + 4 * k
            parts.append(
                jnp.concatenate(
                    [jnp.where(here, high, 0.0), jnp.where(here, value - high, 0.0)], 0
                ).astype(BF16)
            )
        sums = dot(parts[0], picks[0], NT) + dot(parts[1], picks[1], NT)
        win_ref[pl.ds(pl.multiple_of(step * 8, 8), 8), :] = sums[0:8] + sums[8:16]
        return carry

    lax.fori_loop(0, AZ // 2, pair, 0)


def slot_rows(tile_ref, row_ref, pick_ref, mark_ref, devices):
    tile = tile_ref[...].astype(F32)
    line_s, line_l = iota((AZ, AZ), 0), iota((AZ, AZ), 1)
    tile_col = jnp.sum(jnp.where(line_s == line_l, tile, 0.0), 1, keepdims=True)
    same = (tile_col == tile) & (line_l < line_s)
    earlier = jnp.sum(jnp.where(same, 1.0, 0.0), 1, keepdims=True)
    row_col = jnp.sum(jnp.where(line_s == line_l, row_ref[...].astype(F32), 0.0), 1, keepdims=True)
    wide = (AZ, AZ * 4)
    mine = iota(wide, 1) // 4 == iota(wide, 0)
    code = jnp.sum(jnp.where(mine, tile_col * 8.0 + earlier * 4.0, 0.0), 0, keepdims=True)
    code = code + (iota((1, AZ * 4), 1) % 4).astype(F32)
    out = iota((devices * 8, AZ * 4), 0).astype(F32)
    pick_ref[...] = onehot(out == code)
    marks = jnp.where(iota((AZ * 4, AZ), 0) // 4 == iota((AZ * 4, AZ), 1), 1.0, 0.0).astype(BF16)
    spread = jnp.broadcast_to(row_col + 1.0, (AZ, 128)).astype(BF16)
    mark_ref[...] = dot(marks, spread).astype(BF16)


def device_kernel(devices, x_ref, ksmall_ref, k2_ref, k3_ref, geo_ref, cell_ref, tile_ref, row_ref,
                  frac_ref, send_ref, w1_ref, w2_ref, w3_ref, w4_ref, xs_ref, ha_ref, hb_ref,
                  logit_ref, win_ref, pick_ref, mark_ref):
    me = lax.axis_index("tx") * lax.axis_size("ty") + lax.axis_index("ty")
    build_weights(ksmall_ref, k2_ref, k3_ref, w1_ref, w2_ref, w3_ref, w4_ref)
    slot_rows(tile_ref, row_ref, pick_ref, mark_ref, devices)
    line_sums(geo_ref, cell_ref, win_ref)
    covered = jnp.concatenate([win_ref[...].astype(BF16), mark_ref[...]], 1)
    placed = dot(pick_ref[...], covered)
    send_ref[:, 8:16, :] = placed[:, 0:128].reshape(devices, 8, 128).astype(BF16)
    send_ref[:, 16:24, :] = placed[:, 128:256].reshape(devices, 8, 128).astype(BF16)
    conv_layers(x_ref, xs_ref, w1_ref, w2_ref, w3_ref, w4_ref, ha_ref, hb_ref,
                me == 0, me == devices - 1)
    last_layer(w4_ref, ha_ref, logit_ref)
    fraction = (1.0 / (1.0 + jnp.exp(-logit_ref[...]))).astype(BF16)
    frac_ref[...] = fraction
    logit_ref[...] = fraction.astype(F32) * geo_ref[...]
    line_sums(logit_ref, cell_ref, win_ref)
    placed = dot(pick_ref[...], win_ref[...].astype(BF16))
    send_ref[:, 0:8, :] = placed.reshape(devices, 8, 128).astype(BF16)


def build_placer(marks, placer_ref, devices):
    total = devices * 8
    row = iota((TILE, 128), 0).astype(F32)
    inner = iota((128, 128), 0)
    for chunk in range(total // 128):
        part = marks[chunk * 16 : (chunk + 1) * 16].astype(F32).reshape(128, 128)
        part = jnp.sum(jnp.where(inner == iota((128, 128), 1), part, 0.0), 0, keepdims=True)
        lane = iota((1, 128), 1)
        at = jnp.where(part > 0.5, part - 1.0 + ((lane // 2) % 2).astype(F32), -9.0)
        for half in range(2):
            hit = (row == at) & (lane % 2 == half)
            placer_ref[half * TILE : (half + 1) * TILE, chunk * 128 : (chunk + 1) * 128] = onehot(hit)


def tile_kernel(devices, got_ref, depth_ref, level_ref, placer_ref):
    build_placer(got_ref[:, 16:24, :], placer_ref, devices)
    parts = []
    for k in range(2):
        got = got_ref[:, k * 8 : (k + 1) * 8, :].astype(F32).reshape(devices * 8, 128).astype(BF16)
        parts.append(dot(placer_ref[...], got))
    for half in range(2):
        observed = parts[0][half * TILE : (half + 1) * TILE]
        covered = parts[1][half * TILE : (half + 1) * TILE]
        depth = depth_ref[:, half * 128 : (half + 1) * 128]
        wet = depth / (depth + WET_DEPTH)
        innovation = (observed - covered * wet) / (covered + 1.0)
        level_ref[:, half * 128 : (half + 1) * 128] = depth * jnp.exp(innovation)


def flow_steps(level_ref, conv_ref, rain_ref, dirs_ref, runoff_ref):
    def step(count, carry):
        for at in range(0, EXT_ROWS, 16):
            level = level_ref[at : at + 16, :]
            power = jnp.exp2(jnp.log2(jnp.abs(level)) * (2.0 / 3.0))
            runoff_ref[DEPTH + at : DEPTH + at + 16, :] = conv_ref[at : at + 16, :] * level * power
        runoff_ref[0:DEPTH, :] = runoff_ref[EXT_ROWS : EXT_ROWS + DEPTH, :]
        runoff_ref[EXT_ROWS + DEPTH :, :] = runoff_ref[DEPTH : 2 * DEPTH, :]
        for at in range(0, EXT_ROWS, 16):
            rows = [runoff_ref[DEPTH + at - dr : DEPTH + at - dr + 16, :] for dr in (-1, 0, 1)]
            dirs = [dirs_ref[k, at : at + 16, :] for k in range(3)]

            def take(k, code):
                return jnp.where(dirs[k] == code, rows[k], 0.0)

            left = take(0, 0) + take(1, 3) + take(2, 5)
            straight = take(0, 1) + take(2, 6)
            right = take(0, 2) + take(1, 4) + take(2, 7)
            gained = straight + pltpu.roll(right, 1, 1) + pltpu.roll(left, EXT_COLS - 1, 1)
            here = slice(at, at + 16)
            level_ref[here, :] = level_ref[here, :] + rain_ref[here, :] - rows[1] + gained
        return carry

    lax.fori_loop(0, SUBSTEPS, step, 0)


def flow_kernel(field_ref, out_ref, level_ref, conv_ref, rain_ref, dirs_ref, runoff_ref):
    level_ref[...] = field_ref[0]
    conv_ref[...] = RUNOFF_COEF * jnp.sqrt(field_ref[1])
    rain_ref[...] = field_ref[2]
    direction = field_ref[3].astype(I32)
    dirs_ref[0] = pltpu.roll(direction, EXT_ROWS - 1, 0)
    dirs_ref[1] = direction
    dirs_ref[2] = pltpu.roll(direction, 1, 0)
    flow_steps(level_ref, conv_ref, rain_ref, dirs_ref, runoff_ref)
    out_ref[...] = level_ref[...]


def shift_pair(x, axis, dim, width):
    size, length = lax.axis_size(axis), x.shape[dim]
    up = [(i, (i + 1) % size) for i in range(size - 1)]
    down = [(j, i) for i, j in up]
    before = lax.ppermute(lax.slice_in_dim(x, length - width, length, axis=dim), axis, up)
    after = lax.ppermute(lax.slice_in_dim(x, 0, width, axis=dim), axis, down)
    return before, after


def per_device(sar_image, kernel_first, kernel_second, kernel_third, kernel_last, geo_weight,
               cell_index, block_tile, block_row, depth, slope, flow_dir, rain):
    devices = lax.axis_size(("tx", "ty"))
    ksmall = jnp.concatenate(
        [
            kernel_first.transpose(2, 3, 1, 0).reshape(18, 16),
            kernel_last.transpose(0, 2, 3, 1).reshape(9, 16),
            jnp.zeros((5, 16), BF16),
        ],
        0,
    )
    k2 = kernel_second.transpose(2, 3, 0, 1).reshape(144, 16)
    k3 = kernel_third.transpose(2, 3, 0, 1).reshape(144, 16)
    before, after = shift_pair(sar_image, ("tx", "ty"), 1, HALO)
    image = jnp.concatenate(
        [before, sar_image, after, jnp.zeros((2, IMG_ROWS - AZ - 2 * HALO, PX), BF16)], 1
    )
    vmem = pl.BlockSpec(memory_space=pltpu.VMEM)
    fraction, send = pl.pallas_call(
        functools.partial(device_kernel, devices),
        name="swath",
        out_shape=(
            jax.ShapeDtypeStruct((AZ, PX), BF16),
            jax.ShapeDtypeStruct((devices, 24, 128), BF16),
        ),
        in_specs=[vmem] * 8,
        out_specs=(vmem, vmem),
        scratch_shapes=[
            pltpu.VMEM((256, 192), BF16),
            pltpu.VMEM((3, 224, 256), BF16),
            pltpu.VMEM((3, 224, 256), BF16),
            pltpu.VMEM((24, 256), F32),
            pltpu.VMEM((3, 2 * IMG_ROWS, PX), BF16),
            pltpu.VMEM((3, ROWS1 * 16, PX), BF16),
            pltpu.VMEM((3, ROWS1 * 16, PX), BF16),
            pltpu.VMEM((AZ, PX), F32),
            pltpu.VMEM((AZ * 4, 128), F32),
            pltpu.VMEM((devices * 8, AZ * 4), BF16),
            pltpu.VMEM((AZ * 4, 128), BF16),
        ],
    )(image, ksmall, k2, k3, geo_weight, cell_index, block_tile.reshape(1, AZ),
      block_row.reshape(1, AZ))
    got = lax.all_to_all(send, ("tx", "ty"), split_axis=0, concat_axis=0, tiled=True)
    level = pl.pallas_call(
        functools.partial(tile_kernel, devices),
        name="tile",
        out_shape=jax.ShapeDtypeStruct((TILE, TILE), F32),
        in_specs=[vmem] * 2,
        out_specs=vmem,
        scratch_shapes=[pltpu.VMEM((2 * TILE, devices * 8), BF16)],
    )(got, depth)
    fields = jnp.stack([level, slope, rain, flow_dir.astype(F32)])
    before, after = shift_pair(fields, "tx", 1, DEPTH)
    fields = jnp.concatenate([before, fields, after], 1)
    before, after = shift_pair(fields, "ty", 2, DEPTH)
    fill = jnp.zeros((4, EXT_ROWS, EXT_COLS - TILE - 2 * DEPTH), F32)
    fields = jnp.concatenate([before, fields, after, fill], 2)
    level = pl.pallas_call(
        flow_kernel,
        name="flow",
        out_shape=jax.ShapeDtypeStruct((EXT_ROWS, EXT_COLS), F32),
        in_specs=[vmem],
        out_specs=vmem,
        scratch_shapes=[
            pltpu.VMEM((EXT_ROWS, EXT_COLS), F32),
            pltpu.VMEM((EXT_ROWS, EXT_COLS), F32),
            pltpu.VMEM((EXT_ROWS, EXT_COLS), F32),
            pltpu.VMEM((3, EXT_ROWS, EXT_COLS), I32),
            pltpu.VMEM((EXT_ROWS + 2 * DEPTH, EXT_COLS), F32),
        ],
    )(fields)
    return fraction, level[DEPTH : DEPTH + TILE, DEPTH : DEPTH + TILE]


def solution(mesh):
    lines = P(("tx", "ty"), None)
    tiles = P("tx", "ty")
    return jax.shard_map(
        per_device,
        mesh=mesh,
        in_specs=(P(None, ("tx", "ty"), None), P(), P(), P(), P(), lines, lines, lines, lines,
                  tiles, tiles, tiles, tiles),
        out_specs=(lines, tiles),
        check_vma=False,
    )
```

time: 414 us -> 99.4 us (0.24)
  the two profiles are of different devices: /device:TPU:7 before, /device:TPU:1 now
where the time goes in v1:
time: 99.4 us; the launch traced here: 97.9 us
  Pallas kernels  32.7 us (33%)
  starting transfers between devices  29.2 us (29%)
  waiting for transfers between devices  23 us (23%)
  local copies, waits for them, and re-layouts  6.26 us (6%)
  other arithmetic  5.98 us (6%)
    pallas_call x1, Pallas kernels, per_device(): pl.pallas_call(functools.partial(device_kernel, devices), name='swath', o...  22.3 us
    all_to_all x1, waiting for transfers between devices, per_device(): lax.all_to_all(send, ('tx', 'ty'), split_axis=0, concat_axis=0, tiled=True)  16.2 us
    all_to_all x1, starting transfers between devices, per_device(): lax.all_to_all(send, ('tx', 'ty'), split_axis=0, concat_axis=0, tiled=True)  13.3 us
    ppermute x3, starting transfers between devices, shift_pair(): lax.ppermute(lax.slice_in_dim(x, length - width, length, axis=dim), axis,...  10.2 us
    pallas_call x1, Pallas kernels, per_device(): pl.pallas_call(flow_kernel, name='flow', out_shape=jax.ShapeDtypeStruct((...  7.75 us
    ppermute x3, waiting for transfers between devices, shift_pair(): after = lax.ppermute(lax.slice_in_dim(x, 0, width, axis=dim), axis, down)  6.8 us
    ppermute x3, starting transfers between devices, shift_pair(): after = lax.ppermute(lax.slice_in_dim(x, 0, width, axis=dim), axis, down)  5.66 us
    pallas_call x1, Pallas kernels, per_device(): pl.pallas_call(functools.partial(tile_kernel, devices), name='tile', out_...  2.66 us
  transfers between devices with their start and end apart: 7, of which 4 were waited for; matrix products, arithmetic and copies ran while one was open for 3% of the time, Pallas kernels for 0%

profile of v1, /device:TPU:1, one launch (start us, length us, event | category | flops | bytes accessed | tf_op | source)
XLA Modules:
  0.0 97.9 jit_solution(16785365954405535779)
XLA Ops:
  0.6 0.8 fusion.1
  1.4 4.6 %collective-permute-start = (bf16[2,4,512]{2,1,0:T(4,128)(2,1)S(1)}, bf16[2,4,512]{2,1,0:T(4,128)(2,1)S(1)}, u32[]{:S(2)}, u32[]{:S(2)}) collective-permute-start(bf16[2,4,512]{2,1,0:T(4,128)(2,1)S(1)} %get-tuple-element.10), channel_id=1, source_target_pairs={{0,1},{1,2},{2,3},{3,4},{4,5},{5,6},{6,7},{7,8},{8,9},{9,10},{10,1... | collective-permute-start | bytes 24584 | tf_op jit(solution)/shard_map/ppermute | solution.py:283
  6.0 1.9 %collective-permute-start.1 = (bf16[2,4,512]{2,1,0:T(4,128)(2,1)S(1)}, bf16[2,4,512]{2,1,0:T(4,128)(2,1)S(1)}, u32[]{:S(2)}, u32[]{:S(2)}) collective-permute-start(bf16[2,4,512]{2,1,0:T(4,128)(2,1)S(1)} %get-tuple-element.11), channel_id=1, source_target_pairs={{1,0},{2,1},{3,2},{4,3},{5,4},{6,5},{7,6},{8,7},{9,8},{10,9},{11,1... | collective-permute-start | bytes 24584 | tf_op jit(solution)/shard_map/ppermute | solution.py:284
  8.0 0.7 reshape.23
  8.7 0.7 reshape.22
  9.4 0.1 pad.21.clone
  9.4 0.7 maximum_maximum_fusion.2.ksmall_ref
  10.1 0.1 pad.25.clone
  10.2 0.8 collective-permute-done.1
  11.0 1.7 %maximum_maximum_fusion.1.x_ref = bf16[2,96,512]{2,1,0:T(8,128)(2,1)} fusion(bf16[2,4,512]{2,1,0:T(4,128)(2,1)S(1)} %collective-permute-done.1, bf16[2,64,512]{2,1,0:T(8,128)(2,1)} %param.13, bf16[2,4,512]{2,1,0:T(4,128)(2,1)S(1)} %collective-permute-done, bf16[96]{0:T(256)(128)(2,1)S(1)} %pad.25.clone), kind=kLoop, calls=%fused_computation.3 | loop fusion | flops 786432 | bytes 344256 | tf_op jit(solution)/shard_map/concatenate | solution.py:302
  12.7 22.3 %swath.1 = (bf16[64,512]{1,0:T(8,128)(2,1)}, bf16[128,24,128]{2,1,0:T(8,128)(2,1)}) custom-call(bf16[2,96,512]{2,1,0:T(8,128)(2,1)} %maximum_maximum_fusion.1.x_ref, bf16[32,16]{1,0:T(8,128)(2,1)} %maximum_maximum_fusion.2.ksmall_ref, bf16[144,16]{1,0:T(8,128)(2,1)} %bitcast.24, bf16[144,16]{1,0:T(8,128)(2,1)} %bitcast.25, f32[64,512]{1,0:T(8,128)} %geo_ref.1, ...), custom_call_target="tpu_custom_call" | custom-call | tf_op jit(solution)/shard_map/swath/pallas_call | solution.py:306
  35.0 13.3 %all-to-all-start = ((bf16[128,24,128]{2,1,0:T(8,128)(2,1)}), bf16[128,24,128]{2,1,0:T(8,128)(2,1)S(1)}, u32[]{:S(2)}, u32[]{:S(2)}) async-start(bf16[128,24,128]{2,1,0:T(8,128)(2,1)} %get-tuple-element.5), calls=%async_computation | async-start | bytes 1572864 | tf_op jit(solution)/shard_map/all_to_all | solution.py:330
  48.4 16.2 %all-to-all-done.got_ref = bf16[128,24,128]{2,1,0:T(8,128)(2,1)S(1)} async-done(((bf16[128,24,128]{2,1,0:T(8,128)(2,1)}), bf16[128,24,128]{2,1,0:T(8,128)(2,1)S(1)}, u32[]{:S(2)}, u32[]{:S(2)}) %all-to-all-start) | async-done | bytes 786464 | tf_op jit(solution)/shard_map/all_to_all | solution.py:330
  64.5 0.9 copy-done.1
  65.4 2.7 %tile.1 = f32[256,256]{1,0:T(8,128)} custom-call(bf16[128,24,128]{2,1,0:T(8,128)(2,1)} %copy-done.1, f32[256,256]{1,0:T(8,128)} %depth_ref.1), custom_call_target="tpu_custom_call" | custom-call | tf_op jit(solution)/shard_map/tile/pallas_call | solution.py:331
  68.1 0.7 pad_maximum_fusion.4
  68.8 2.1 %collective-permute-start.2 = (f32[4,8,256]{2,1,0:T(8,128)S(1)}, f32[4,8,256]{2,1,0:T(8,128)S(1)}, u32[]{:S(2)}, u32[]{:S(2)}) collective-permute-start(f32[4,8,256]{2,1,0:T(8,128)S(1)} %get-tuple-element.8), channel_id=1, source_target_pairs={{0,8},{8,16},{16,24},{24,32},{32,40},{40,48},{48,56},{56,64},{64,7... | collective-permute-start | bytes 98312 | tf_op jit(solution)/shard_map/ppermute | solution.py:283
  71.0 1.3 %collective-permute-start.3 = (f32[4,8,256]{2,1,0:T(8,128)S(1)}, f32[4,8,256]{2,1,0:T(8,128)S(1)}, u32[]{:S(2)}, u32[]{:S(2)}) collective-permute-start(f32[4,8,256]{2,1,0:T(8,128)S(1)} %get-tuple-element.9), channel_id=1, source_target_pairs={{8,0},{16,8},{24,16},{32,24},{40,32},{48,40},{56,48},{64,56},{72,6... | collective-permute-start | bytes 98312 | tf_op jit(solution)/shard_map/ppermute | solution.py:284
  72.3 3.3 %collective-permute-done.3 = f32[4,8,256]{2,1,0:T(8,128)S(1)} collective-permute-done((f32[4,8,256]{2,1,0:T(8,128)S(1)}, f32[4,8,256]{2,1,0:T(8,128)S(1)}, u32[]{:S(2)}, u32[]{:S(2)}) %collective-permute-start.3) | collective-permute-done | bytes 32800 | tf_op jit(solution)/shard_map/ppermute | solution.py:284
  75.6 1.0 %pad_maximum_fusion = f32[4,272,256]{2,1,0:T(8,128)S(1)} fusion(f32[4,8,256]{2,1,0:T(8,128)S(1)} %collective-permute-done.3, f32[1,256,256]{2,1,0:T(8,128)S(1)} %convert_bitcast_fusion, f32[1,256,256]{2,1,0:T(8,128)S(1)} %bitcast.19, f32[1,256,256]{2,1,0:T(8,128)S(1)} %bitcast.22, f32[1,256,256]{2,1,0:T(8,128)} %bitcast.16, ...), kind=kLoop, calls=%fused_computation.1 | loop fusion | flops 1392640 | bytes 2228224 | tf_op jit(solution)/shard_map/concatenate | solution.py:341
  76.7 0.2 fusion
  76.9 0.2 copy.15
  77.1 3.4 %collective-permute-start.4 = (f32[4,272,8]{1,2,0:T(8,128)S(1)}, f32[4,272,8]{1,2,0:T(8,128)S(1)}, u32[]{:S(2)}, u32[]{:S(2)}) collective-permute-start(f32[4,272,8]{1,2,0:T(8,128)S(1)} %copy.15), channel_id=1, source_target_pairs={{0,1},{1,2},{2,3},{3,4},{4,5},{5,6},{6,7},{8,9},{9,10},{10,11},{11... | collective-permute-start | bytes 104456 | tf_op jit(solution)/shard_map/ppermute | solution.py:283
  80.6 0.2 copy.16
  80.8 2.4 %collective-permute-start.5 = (f32[4,272,8]{1,2,0:T(8,128)S(1)}, f32[4,272,8]{1,2,0:T(8,128)S(1)}, u32[]{:S(2)}, u32[]{:S(2)}) collective-permute-start(f32[4,272,8]{1,2,0:T(8,128)S(1)} %copy.16), channel_id=1, source_target_pairs={{1,0},{2,1},{3,2},{4,3},{5,4},{6,5},{7,6},{9,8},{10,9},{11,10},{12... | collective-permute-start | bytes 104456 | tf_op jit(solution)/shard_map/ppermute | solution.py:284
  83.3 0.1 pad.8.clone
  83.4 0.2 copy.17
  83.6 2.7 %collective-permute-done.5 = f32[4,272,8]{1,2,0:T(8,128)S(1)} collective-permute-done((f32[4,272,8]{1,2,0:T(8,128)S(1)}, f32[4,272,8]{1,2,0:T(8,128)S(1)}, u32[]{:S(2)}, u32[]{:S(2)}) %collective-permute-start.5) | collective-permute-done | bytes 34848 | tf_op jit(solution)/shard_map/ppermute | solution.py:284
  86.2 0.2 copy.18
  86.5 1.8 %maximum_maximum_fusion.field_ref = f32[4,272,384]{2,1,0:T(8,128)} fusion(f32[4,272,8]{2,1,0:T(8,128)S(1)} %copy.18, f32[4,8,256]{2,1,0:T(8,128)S(1)} %collective-permute-done.3, f32[1,256,256]{2,1,0:T(8,128)S(1)} %convert_bitcast_fusion, f32[1,256,256]{2,1,0:T(8,128)S(1)} %bitcast.20, f32[1,256,256]{2,1,0:T(8,128)S(1)} %bitcast.23, ...), kind=kLoop, calls=%fused_computation | loop fusion | flops 3342336 | bytes 2856448 | tf_op jit(solution)/shard_map/concatenate | solution.py:344
  88.3 7.8 %flow.1 = f32[272,384]{1,0:T(8,128)} custom-call(f32[4,272,384]{2,1,0:T(8,128)} %maximum_maximum_fusion.field_ref), custom_call_target="tpu_custom_call" | custom-call | tf_op jit(solution)/shard_map/flow/pallas_call | solution.py:345
  96.0 1.8 %slice.30 = f32[256,256]{1,0:T(8,128)} slice(f32[272,384]{1,0:T(8,128)} %flow.1), slice={[8:264], [8:264]} | slice | bytes 524288 | tf_op jit(solution)/shard_map/slice | solution.py:359
  (16 shorter events, 0.1 us)
Async XLA Ops:
  0.6 47.7 %copy-start.4 = (s32[256,256]{1,0:T(8,128)S(1)}, s32[256,256]{1,0:T(8,128)}, u32[]{:S(2)}) copy-start(s32[256,256]{1,0:T(8,128)} %param.24) | copy-start | bytes 786436
  1.4 8.8 %collective-permute-start = (bf16[2,4,512]{2,1,0:T(4,128)(2,1)S(1)}, bf16[2,4,512]{2,1,0:T(4,128)(2,1)S(1)}, u32[]{:S(2)}, u32[]{:S(2)}) collective-permute-start(bf16[2,4,512]{2,1,0:T(4,128)(2,1)S(1)} %get-tuple-element.10), channel_id=1, source_target_pairs={{0,1},{1,2},{2,3},{3,4},{4,5},{5,6},{6,7},{7,8},{8,9},{9,10},{10,1... | collective-permute-start | bytes 24584 | tf_op jit(solution)/shard_map/ppermute | solution.py:283
  6.0 5.0 %collective-permute-start.1 = (bf16[2,4,512]{2,1,0:T(4,128)(2,1)S(1)}, bf16[2,4,512]{2,1,0:T(4,128)(2,1)S(1)}, u32[]{:S(2)}, u32[]{:S(2)}) collective-permute-start(bf16[2,4,512]{2,1,0:T(4,128)(2,1)S(1)} %get-tuple-element.11), channel_id=1, source_target_pairs={{1,0},{2,1},{3,2},{4,3},{5,4},{6,5},{7,6},{8,7},{9,8},{10,9},{11,1... | collective-permute-start | bytes 24584 | tf_op jit(solution)/shard_map/ppermute | solution.py:284
  35.0 33.1 %copy-start.2 = (f32[256,256]{1,0:T(8,128)S(1)}, f32[256,256]{1,0:T(8,128)}, u32[]{:S(2)}) copy-start(f32[256,256]{1,0:T(8,128)} %param.25) | copy-start | bytes 786436
  35.0 33.1 %copy-start.3 = (f32[256,256]{1,0:T(8,128)S(1)}, f32[256,256]{1,0:T(8,128)}, u32[]{:S(2)}) copy-start(f32[256,256]{1,0:T(8,128)} %param.23) | copy-start | bytes 786436
  35.0 29.6 %all-to-all-start = ((bf16[128,24,128]{2,1,0:T(8,128)(2,1)}), bf16[128,24,128]{2,1,0:T(8,128)(2,1)S(1)}, u32[]{:S(2)}, u32[]{:S(2)}) async-start(bf16[128,24,128]{2,1,0:T(8,128)(2,1)} %get-tuple-element.5), calls=%async_computation | async-start | bytes 1572864 | tf_op jit(solution)/shard_map/all_to_all | solution.py:330
  64.5 0.9 copy-start.1
  68.8 3.4 %collective-permute-start.2 = (f32[4,8,256]{2,1,0:T(8,128)S(1)}, f32[4,8,256]{2,1,0:T(8,128)S(1)}, u32[]{:S(2)}, u32[]{:S(2)}) collective-permute-start(f32[4,8,256]{2,1,0:T(8,128)S(1)} %get-tuple-element.8), channel_id=1, source_target_pairs={{0,8},{8,16},{16,24},{24,32},{32,40},{40,48},{48,56},{56,64},{64,7... | collective-permute-start | bytes 98312 | tf_op jit(solution)/shard_map/ppermute | solution.py:283
  71.0 4.7 %collective-permute-start.3 = (f32[4,8,256]{2,1,0:T(8,128)S(1)}, f32[4,8,256]{2,1,0:T(8,128)S(1)}, u32[]{:S(2)}, u32[]{:S(2)}) collective-permute-start(f32[4,8,256]{2,1,0:T(8,128)S(1)} %get-tuple-element.9), channel_id=1, source_target_pairs={{8,0},{16,8},{24,16},{32,24},{40,32},{48,40},{56,48},{64,56},{72,6... | collective-permute-start | bytes 98312 | tf_op jit(solution)/shard_map/ppermute | solution.py:284
  76.9 9.5 %copy-start = (f32[256,256]{1,0:T(8,128)S(1)}, f32[256,256]{1,0:T(8,128)}, u32[]{:S(2)}) copy-start(f32[256,256]{1,0:T(8,128)} %tile.1) | copy-start | bytes 786436
  77.1 6.2 %collective-permute-start.4 = (f32[4,272,8]{1,2,0:T(8,128)S(1)}, f32[4,272,8]{1,2,0:T(8,128)S(1)}, u32[]{:S(2)}, u32[]{:S(2)}) collective-permute-start(f32[4,272,8]{1,2,0:T(8,128)S(1)} %copy.15), channel_id=1, source_target_pairs={{0,1},{1,2},{2,3},{3,4},{4,5},{5,6},{6,7},{8,9},{9,10},{10,11},{11... | collective-permute-start | bytes 104456 | tf_op jit(solution)/shard_map/ppermute | solution.py:283
  80.8 5.4 %collective-permute-start.5 = (f32[4,272,8]{1,2,0:T(8,128)S(1)}, f32[4,272,8]{1,2,0:T(8,128)S(1)}, u32[]{:S(2)}, u32[]{:S(2)}) collective-permute-start(f32[4,272,8]{1,2,0:T(8,128)S(1)} %copy.16), channel_id=1, source_target_pairs={{1,0},{2,1},{3,2},{4,3},{5,4},{6,5},{7,6},{9,8},{10,9},{11,10},{12... | collective-permute-start | bytes 104456 | tf_op jit(solution)/shard_map/ppermute | solution.py:284

commit v2 on v1

--- a/solution.py
+++ b/solution.py
@@ -21,13 +21,16 @@
 AZ = 64
 PX = 512
 HALO = 4
+SIDE = 8
 IMG_ROWS = 96
 ROWS1 = 80
 TILE = 256
 DEPTH = 8
 EXT_ROWS = TILE + 2 * DEPTH
 EXT_COLS = TILE + 128
-
+CORNERS = ((1, 1), (1, -1), (-1, 1), (-1, -1))
+
+MESH = pl.DeviceIdType.MESH
 NN = (((1,), (0,)), ((), ()))
 NT = (((1,), (1,)), ((), ()))
 TN = (((0,), (0,)), ((), ()))
@@ -73,7 +76,7 @@
     for row in range(16):
         value = jnp.zeros((16, 192), F32)
         for dy in range(3):
-            value = jnp.where(in_row == row + dy, taps[dy], value)
+            value = jnp.where(in_row == row + dy + SIDE - HALO, taps[dy], value)
         w1_ref[row * 16 : (row + 1) * 16, :] = value.astype(BF16)
     tiled = dot(ksmall_ref[...], spread)
     band = iota((8, 256), 1) // 16 - iota((8, 256), 0)
@@ -100,9 +103,12 @@
             h_ref[:, start * 16 : (start + width) * 16, :] = jnp.zeros((3, width * 16, PX), BF16)
 
 
-def conv_layers(x_ref, xs_ref, w1_ref, w2_ref, w3_ref, w4_ref, ha_ref, hb_ref, first, last):
+def conv_layers(x_ref, side_ref, xs_ref, w1_ref, w2_ref, w3_ref, ha_ref, hb_ref, first, last):
     for pol in range(2):
-        value = x_ref[pol].astype(F32)
+        before = jnp.where(first, 0.0, side_ref[0, pol].astype(F32))
+        after = jnp.where(last, 0.0, side_ref[1, pol].astype(F32))
+        fill = jnp.zeros((IMG_ROWS - AZ - 2 * SIDE, PX), F32)
+        value = jnp.concatenate([before, x_ref[pol].astype(F32), after, fill], 0)
         base = pol * IMG_ROWS
         xs_ref[1, base : base + IMG_ROWS, :] = value.astype(BF16)
         xs_ref[0, base : base + IMG_ROWS, :] = shifted(value, 1).astype(BF16)
@@ -187,28 +193,6 @@
     mark_ref[...] = dot(marks, spread).astype(BF16)
 
 
-def device_kernel(devices, x_ref, ksmall_ref, k2_ref, k3_ref, geo_ref, cell_ref, tile_ref, row_ref,
-                  frac_ref, send_ref, w1_ref, w2_ref, w3_ref, w4_ref, xs_ref, ha_ref, hb_ref,
-                  logit_ref, win_ref, pick_ref, mark_ref):
-    me = lax.axis_index("tx") * lax.axis_size("ty") + lax.axis_index("ty")
-    build_weights(ksmall_ref, k2_ref, k3_ref, w1_ref, w2_ref, w3_ref, w4_ref)
-    slot_rows(tile_ref, row_ref, pick_ref, mark_ref, devices)
-    line_sums(geo_ref, cell_ref, win_ref)
-    covered = jnp.concatenate([win_ref[...].astype(BF16), mark_ref[...]], 1)
-    placed = dot(pick_ref[...], covered)
-    send_ref[:, 8:16, :] = placed[:, 0:128].reshape(devices, 8, 128).astype(BF16)
-    send_ref[:, 16:24, :] = placed[:, 128:256].reshape(devices, 8, 128).astype(BF16)
-    conv_layers(x_ref, xs_ref, w1_ref, w2_ref, w3_ref, w4_ref, ha_ref, hb_ref,
-                me == 0, me == devices - 1)
-    last_layer(w4_ref, ha_ref, logit_ref)
-    fraction = (1.0 / (1.0 + jnp.exp(-logit_ref[...]))).astype(BF16)
-    frac_ref[...] = fraction
-    logit_ref[...] = fraction.astype(F32) * geo_ref[...]
-    line_sums(logit_ref, cell_ref, win_ref)
-    placed = dot(pick_ref[...], win_ref[...].astype(BF16))
-    send_ref[:, 0:8, :] = placed.reshape(devices, 8, 128).astype(BF16)
-
-
 def build_placer(marks, placer_ref, devices):
     total = devices * 8
     row = iota((TILE, 128), 0).astype(F32)
@@ -223,21 +207,6 @@
             placer_ref[half * TILE : (half + 1) * TILE, chunk * 128 : (chunk + 1) * 128] = onehot(hit)
 
 
-def tile_kernel(devices, got_ref, depth_ref, level_ref, placer_ref):
-    build_placer(got_ref[:, 16:24, :], placer_ref, devices)
-    parts = []
-    for k in range(2):
-        got = got_ref[:, k * 8 : (k + 1) * 8, :].astype(F32).reshape(devices * 8, 128).astype(BF16)
-        parts.append(dot(placer_ref[...], got))
-    for half in range(2):
-        observed = parts[0][half * TILE : (half + 1) * TILE]
-        covered = parts[1][half * TILE : (half + 1) * TILE]
-        depth = depth_ref[:, half * 128 : (half + 1) * 128]
-        wet = depth / (depth + WET_DEPTH)
-        innovation = (observed - covered * wet) / (covered + 1.0)
-        level_ref[:, half * 128 : (half + 1) * 128] = depth * jnp.exp(innovation)
-
-
 def flow_steps(level_ref, conv_ref, rain_ref, dirs_ref, runoff_ref):
     def step(count, carry):
         for at in range(0, EXT_ROWS, 16):
@@ -264,30 +233,227 @@
     lax.fori_loop(0, SUBSTEPS, step, 0)
 
 
-def flow_kernel(field_ref, out_ref, level_ref, conv_ref, rain_ref, dirs_ref, runoff_ref):
-    level_ref[...] = field_ref[0]
-    conv_ref[...] = RUNOFF_COEF * jnp.sqrt(field_ref[1])
-    rain_ref[...] = field_ref[2]
-    direction = field_ref[3].astype(I32)
-    dirs_ref[0] = pltpu.roll(direction, EXT_ROWS - 1, 0)
-    dirs_ref[1] = direction
-    dirs_ref[2] = pltpu.roll(direction, 1, 0)
+def covered_level(parts, depth_ref, level_ref):
+    for half in range(2):
+        lanes = slice(half * 128, (half + 1) * 128)
+        observed = parts[0][half * TILE : (half + 1) * TILE]
+        covered = parts[1][half * TILE : (half + 1) * TILE]
+        depth = depth_ref[:, lanes]
+        wet = depth / (depth + WET_DEPTH)
+        innovation = (observed - covered * wet) / (covered + 1.0)
+        level_ref[0:TILE, lanes] = depth * jnp.exp(innovation)
+
+
+def pack_columns(block, low):
+    lane = iota((16, 128), 1)
+    packed = jnp.zeros((16, 128), F32)
+    for group in range(16):
+        moved = pltpu.roll(block[group * 16 : (group + 1) * 16], (group * 8 - low) % 128, 1)
+        packed = jnp.where(lane // 8 == group, moved, packed)
+    return packed
+
+
+def unpack_columns(packed_left, packed_right, fill):
+    lane = iota((16, 128), 1)
+    out = []
+    for group in range(16):
+        right = pltpu.roll(packed_right, (-group * 8) % 128, 1)
+        left = pltpu.roll(packed_left, (120 - group * 8) % 128, 1)
+        out.append(jnp.where(lane < 8, right, jnp.where(lane >= 120, left, fill)))
+    return jnp.concatenate(out, 0)
+
+
+def fill_edges(field_ref, index, rows_ref, cols_ref, corners_ref):
+    rows_ref[0, index] = field_ref[TILE - DEPTH : TILE, 0:TILE]
+    rows_ref[1, index] = field_ref[0:DEPTH, 0:TILE]
+    cols_ref[0, index] = pack_columns(field_ref[0:TILE, 128:256], 120)
+    cols_ref[1, index] = pack_columns(field_ref[0:TILE, 0:128], 0)
+    for k, (a, b) in enumerate(CORNERS):
+        rows = slice(TILE - DEPTH, TILE) if a > 0 else slice(0, DEPTH)
+        lanes = slice(128, 256) if b > 0 else slice(0, 128)
+        corners_ref[k, index] = field_ref[rows, lanes]
+
+
+def take_edges(field_ref, index, rows_ref, cols_ref, corners_ref, fill):
+    lane = iota((DEPTH, 128), 1)
+    field_ref[TILE : TILE + DEPTH, 0:TILE] = rows_ref[1, index]
+    field_ref[TILE + DEPTH : EXT_ROWS, 0:TILE] = rows_ref[0, index]
+    field_ref[0:TILE, TILE:EXT_COLS] = unpack_columns(cols_ref[0, index], cols_ref[1, index], fill)
+    for at, down in ((TILE, -1), (TILE + DEPTH, 1)):
+        left = corners_ref[CORNERS.index((down, 1)), index]
+        right = corners_ref[CORNERS.index((down, -1)), index]
+        both = jnp.where(lane < 8, right, jnp.where(lane >= 120, left, fill))
+        field_ref[at : at + DEPTH, TILE:EXT_COLS] = both
+
+
+def edge_copies(place, sent, got, send_sem, recv_sem):
+    tx, ty, n_tx, n_ty = place
+    steps = [((1, 0), 0, 0), ((-1, 0), 0, 1), ((0, 1), 1, 0), ((0, -1), 1, 1)]
+    steps += [(step, 2, k) for k, step in enumerate(CORNERS)]
+    copies = []
+    for number, ((a, b), which, k) in enumerate(steps):
+        copies.append(
+            pltpu.make_async_remote_copy(
+                src_ref=sent[which].at[k],
+                dst_ref=got[which].at[k],
+                send_sem=send_sem.at[number],
+                recv_sem=recv_sem.at[number],
+                device_id=(lax.rem(tx + a + n_tx, n_tx), lax.rem(ty + b + n_ty, n_ty)),
+                device_id_type=MESH,
+            )
+        )
+    return copies
+
+
+def exchange(me, devices, n_ty, sent_ref, got_ref, own_sem, send_sem, recv_sem):
+    own = pltpu.make_async_copy(sent_ref.at[me], got_ref.at[me], own_sem)
+    own.start()
+
+    def send(step, carry):
+        peer = lax.rem(me + step, devices)
+        pltpu.make_async_remote_copy(
+            src_ref=sent_ref.at[peer],
+            dst_ref=got_ref.at[me],
+            send_sem=send_sem,
+            recv_sem=recv_sem,
+            device_id=(peer // n_ty, lax.rem(peer, n_ty)),
+            device_id_type=MESH,
+        ).start()
+        return carry
+
+    lax.fori_loop(1, devices, send, 0)
+    return own
+
+
+def wait_bytes(ref, count, sem):
+    pltpu.make_async_copy(ref.at[pl.ds(0, count)], ref.at[pl.ds(0, count)], sem).wait()
+
+
+def whole_kernel(n_tx, n_ty, *refs):
+    (x_in, ksmall_ref, k2_ref, k3_ref, geo_in, cell_in, tile_ref, row_ref, depth_in, slope_in,
+     dir_in, rain_in, frac_ref, out_ref,
+     x_ref, geo_ref, cell_ref, depth_ref, dir_ref, slope_ref, rain_in_ref, in_sem,
+     w1_ref, w2_ref, w3_ref, w4_ref, side_ref, xs_ref, ha_ref, hb_ref, logit_ref, win_ref,
+     pick_ref, mark_ref, early_ref, early_got, late_ref, late_got, placer_ref,
+     level_ref, conv_ref, rain_ref, dirs_ref, runoff_ref,
+     rows_s, cols_s, corners_s, rows_g, cols_g, corners_g,
+     rows_l, cols_l, corners_l, rows_m, cols_m, corners_m,
+     side_send, side_recv, edge_send, edge_recv, last_send, last_recv,
+     own_sem, early_send, early_recv, late_send, late_recv) = refs
+    devices = n_tx * n_ty
+    tx, ty = lax.axis_index("tx"), lax.axis_index("ty")
+    me = tx * n_ty + ty
+    place = (tx, ty, n_tx, n_ty)
+    barrier = pltpu.get_barrier_semaphore()
+
+    def greet(step, carry):
+        peer = lax.rem(me + step, devices)
+        pl.semaphore_signal(barrier, inc=1, device_id=(peer // n_ty, lax.rem(peer, n_ty)),
+                            device_id_type=MESH)
+        return carry
+
+    lax.fori_loop(1, devices, greet, 0)
+    loads = []
+    for number, (src, dst) in enumerate(
+        ((slope_in, slope_ref), (rain_in, rain_in_ref), (dir_in, dir_ref), (geo_in, geo_ref),
+         (cell_in, cell_ref), (depth_in, depth_ref), (x_in, x_ref))
+    ):
+        loads.append(pltpu.make_async_copy(src, dst, in_sem.at[number]))
+        loads[-1].start()
+    build_weights(ksmall_ref, k2_ref, k3_ref, w1_ref, w2_ref, w3_ref, w4_ref)
+    slot_rows(tile_ref, row_ref, pick_ref, mark_ref, devices)
+    for load in loads:
+        load.wait()
+    conv_ref[0:TILE, 0:TILE] = RUNOFF_COEF * jnp.sqrt(slope_ref[...])
+    rain_ref[0:TILE, 0:TILE] = rain_in_ref[...]
+    dirs_ref[1, 0:TILE, 0:TILE] = dir_ref[...].astype(F32)
+    direction = dirs_ref.at[1]
+    for index, field in enumerate((conv_ref, rain_ref, direction)):
+        fill_edges(field, index, rows_s, cols_s, corners_s)
+    pl.semaphore_wait(barrier, devices - 1)
+
+    sides = []
+    for k, (step, at) in enumerate(((1, AZ - SIDE), (-1, 0))):
+        peer = lax.rem(me + step + devices, devices)
+        sides.append(
+            pltpu.make_async_remote_copy(
+                src_ref=x_ref.at[:, at : at + SIDE, :],
+                dst_ref=side_ref.at[k],
+                send_sem=side_send.at[k],
+                recv_sem=side_recv.at[k],
+                device_id=(peer // n_ty, lax.rem(peer, n_ty)),
+                device_id_type=MESH,
+            )
+        )
+        sides[-1].start()
+    edges = edge_copies(place, (rows_s, cols_s, corners_s), (rows_g, cols_g, corners_g),
+                        edge_send, edge_recv)
+    for copy in edges:
+        copy.start()
+    line_sums(geo_ref, cell_ref, win_ref)
+    covered = jnp.concatenate([win_ref[...].astype(BF16), mark_ref[...]], 1)
+    placed = dot(pick_ref[...], covered)
+    early_ref[:, 0:8, :] = placed[:, 0:128].reshape(devices, 8, 128).astype(BF16)
+    early_ref[:, 8:16, :] = placed[:, 128:256].reshape(devices, 8, 128).astype(BF16)
+    own_early = exchange(me, devices, n_ty, early_ref, early_got, own_sem.at[0], early_send, early_recv)
+
+    for copy in sides:
+        copy.wait()
+    conv_layers(x_ref, side_ref, xs_ref, w1_ref, w2_ref, w3_ref, ha_ref, hb_ref,
+                me == 0, me == devices - 1)
+    last_layer(w4_ref, ha_ref, logit_ref)
+    fraction = (1.0 / (1.0 + jnp.exp(-logit_ref[...]))).astype(BF16)
+    frac_ref[...] = fraction
+    logit_ref[...] = fraction.astype(F32) * geo_ref[...]
+    line_sums(logit_ref, cell_ref, win_ref)
+    placed = dot(pick_ref[...], win_ref[...].astype(BF16))
+    late_ref[...] = placed.reshape(devices, 8, 128).astype(BF16)
+    own_late = exchange(me, devices, n_ty, late_ref, late_got, own_sem.at[1], late_send, late_recv)
+
+    for copy in edges:
+        copy.wait()
+    for index, (field, fill) in enumerate(((conv_ref, 0.0), (rain_ref, 0.0), (direction, 8.0))):
+        take_edges(field, index, rows_g, cols_g, corners_g, fill)
+    for cond, at in ((tx == n_tx - 1, TILE), (tx == 0, TILE + DEPTH)):
+
+        @pl.when(cond)
+        def _():
+            conv_ref[at : at + DEPTH, :] = jnp.zeros((DEPTH, EXT_COLS), F32)
+
+    lane = iota((EXT_ROWS, 128), 1)
+    outside = ((ty == n_ty - 1) & (lane < 64)) | ((ty == 0) & (lane >= 64))
+    conv_ref[:, TILE:EXT_COLS] = jnp.where(outside, 0.0, conv_ref[:, TILE:EXT_COLS])
+    dirs_ref[0] = pltpu.roll(dirs_ref[1], EXT_ROWS - 1, 0)
+    dirs_ref[2] = pltpu.roll(dirs_ref[1], 1, 0)
+    own_early.wait()
+    wait_bytes(early_got, devices - 1, early_recv)
+    build_placer(early_got[:, 8:16, :], placer_ref, devices)
+    parts = [None, None]
+    got = early_got[:, 0:8, :].astype(F32).reshape(devices * 8, 128).astype(BF16)
+    parts[1] = dot(placer_ref[...], got)
+    own_late.wait()
+    wait_bytes(late_got, devices - 1, late_recv)
+    got = late_got[...].astype(F32).reshape(devices * 8, 128).astype(BF16)
+    parts[0] = dot(placer_ref[...], got)
+    covered_level(parts, depth_ref, level_ref)
+
+    fill_edges(level_ref, 0, rows_l, cols_l, corners_l)
+    lasts = edge_copies(place, (rows_l, cols_l, corners_l), (rows_m, cols_m, corners_m),
+                        last_send, last_recv)
+    for copy in lasts:
+        copy.start()
+    wait_bytes(early_ref, devices - 1, early_send)
+    wait_bytes(late_ref, devices - 1, late_send)
+    for copy in lasts:
+        copy.wait()
+    take_edges(level_ref, 0, rows_m, cols_m, corners_m, 0.0)
     flow_steps(level_ref, conv_ref, rain_ref, dirs_ref, runoff_ref)
-    out_ref[...] = level_ref[...]
-
-
-def shift_pair(x, axis, dim, width):
-    size, length = lax.axis_size(axis), x.shape[dim]
-    up = [(i, (i + 1) % size) for i in range(size - 1)]
-    down = [(j, i) for i, j in up]
-    before = lax.ppermute(lax.slice_in_dim(x, length - width, length, axis=dim), axis, up)
-    after = lax.ppermute(lax.slice_in_dim(x, 0, width, axis=dim), axis, down)
-    return before, after
-
-
-def per_device(sar_image, kernel_first, kernel_second, kernel_third, kernel_last, geo_weight,
-               cell_index, block_tile, block_row, depth, slope, flow_dir, rain):
-    devices = lax.axis_size(("tx", "ty"))
+    out_ref[...] = level_ref[0:TILE, 0:TILE]
+
+
+def per_device(n_tx, n_ty, sar_image, kernel_first, kernel_second, kernel_third, kernel_last,
+               geo_weight, cell_index, block_tile, block_row, depth, slope, flow_dir, rain):
+    devices = n_tx * n_ty
     ksmall = jnp.concatenate(
         [
             kernel_first.transpose(2, 3, 1, 0).reshape(18, 16),
@@ -298,25 +464,40 @@
     )
     k2 = kernel_second.transpose(2, 3, 0, 1).reshape(144, 16)
     k3 = kernel_third.transpose(2, 3, 0, 1).reshape(144, 16)
-    before, after = shift_pair(sar_image, ("tx", "ty"), 1, HALO)
-    image = jnp.concatenate(
-        [before, sar_image, after, jnp.zeros((2, IMG_ROWS - AZ - 2 * HALO, PX), BF16)], 1
-    )
     vmem = pl.BlockSpec(memory_space=pltpu.VMEM)
-    fraction, send = pl.pallas_call(
-        functools.partial(device_kernel, devices),
-        name="swath",
+    stay = pl.BlockSpec(memory_space=pl.ANY)
+    dma = pltpu.SemaphoreType.DMA
+
+    def edge_buffers(count):
+        return [
+            pltpu.VMEM((2, count, DEPTH, TILE), F32),
+            pltpu.VMEM((2, count, 16, 128), F32),
+            pltpu.VMEM((4, count, DEPTH, 128), F32),
+        ]
+
+    return pl.pallas_call(
+        functools.partial(whole_kernel, n_tx, n_ty),
+        name="assimilate",
         out_shape=(
             jax.ShapeDtypeStruct((AZ, PX), BF16),
-            jax.ShapeDtypeStruct((devices, 24, 128), BF16),
+            jax.ShapeDtypeStruct((TILE, TILE), F32),
         ),
-        in_specs=[vmem] * 8,
+        in_specs=[stay, vmem, vmem, vmem, stay, stay, vmem, vmem, stay, stay, stay, stay],
         out_specs=(vmem, vmem),
         scratch_shapes=[
+            pltpu.VMEM((2, AZ, PX), BF16),
+            pltpu.VMEM((AZ, PX), F32),
+            pltpu.VMEM((AZ, PX), I32),
+            pltpu.VMEM((TILE, TILE), F32),
+            pltpu.VMEM((TILE, TILE), I32),
+            pltpu.VMEM((TILE, TILE), F32),
+            pltpu.VMEM((TILE, TILE), F32),
+            dma((7,)),
             pltpu.VMEM((256, 192), BF16),
             pltpu.VMEM((3, 224, 256), BF16),
             pltpu.VMEM((3, 224, 256), BF16),
             pltpu.VMEM((24, 256), F32),
+            pltpu.VMEM((2, 2, SIDE, PX), BF16),
             pltpu.VMEM((3, 2 * IMG_ROWS, PX), BF16),
             pltpu.VMEM((3, ROWS1 * 16, PX), BF16),
             pltpu.VMEM((3, ROWS1 * 16, PX), BF16),
@@ -324,46 +505,30 @@
             pltpu.VMEM((AZ * 4, 128), F32),
             pltpu.VMEM((devices * 8, AZ * 4), BF16),
             pltpu.VMEM((AZ * 4, 128), BF16),
-        ],
-    )(image, ksmall, k2, k3, geo_weight, cell_index, block_tile.reshape(1, AZ),
-      block_row.reshape(1, AZ))
-    got = lax.all_to_all(send, ("tx", "ty"), split_axis=0, concat_axis=0, tiled=True)
-    level = pl.pallas_call(
-        functools.partial(tile_kernel, devices),
-        name="tile",
-        out_shape=jax.ShapeDtypeStruct((TILE, TILE), F32),
-        in_specs=[vmem] * 2,
-        out_specs=vmem,
-        scratch_shapes=[pltpu.VMEM((2 * TILE, devices * 8), BF16)],
-    )(got, depth)
-    fields = jnp.stack([level, slope, rain, flow_dir.astype(F32)])
-    before, after = shift_pair(fields, "tx", 1, DEPTH)
-    fields = jnp.concatenate([before, fields, after], 1)
-    before, after = shift_pair(fields, "ty", 2, DEPTH)
-    fill = jnp.zeros((4, EXT_ROWS, EXT_COLS - TILE - 2 * DEPTH), F32)
-    fields = jnp.concatenate([before, fields, after, fill], 2)
-    level = pl.pallas_call(
-        flow_kernel,
-        name="flow",
-        out_shape=jax.ShapeDtypeStruct((EXT_ROWS, EXT_COLS), F32),
-        in_specs=[vmem],
-        out_specs=vmem,
-        scratch_shapes=[
+            pltpu.VMEM((devices, 16, 128), BF16),
+            pltpu.VMEM((devices, 16, 128), BF16),
+            pltpu.VMEM((devices, 8, 128), BF16),
+            pltpu.VMEM((devices, 8, 128), BF16),
+            pltpu.VMEM((2 * TILE, devices * 8), BF16),
             pltpu.VMEM((EXT_ROWS, EXT_COLS), F32),
             pltpu.VMEM((EXT_ROWS, EXT_COLS), F32),
             pltpu.VMEM((EXT_ROWS, EXT_COLS), F32),
-            pltpu.VMEM((3, EXT_ROWS, EXT_COLS), I32),
+            pltpu.VMEM((3, EXT_ROWS, EXT_COLS), F32),
             pltpu.VMEM((EXT_ROWS + 2 * DEPTH, EXT_COLS), F32),
+            *edge_buffers(3), *edge_buffers(3), *edge_buffers(1), *edge_buffers(1),
+            dma((2,)), dma((2,)), dma((8,)), dma((8,)), dma((8,)), dma((8,)),
+            dma((2,)), dma(()), dma(()), dma(()), dma(()),
         ],
-    )(fields)
-    return fraction, level[DEPTH : DEPTH + TILE, DEPTH : DEPTH + TILE]
+        compiler_params=pltpu.CompilerParams(collective_id=0, has_side_effects=True),
+    )(sar_image, ksmall, k2, k3, geo_weight, cell_index, block_tile.reshape(1, AZ),
+      block_row.reshape(1, AZ), depth, slope, flow_dir, rain)
 
 
 def solution(mesh):
     lines = P(("tx", "ty"), None)
     tiles = P("tx", "ty")
     return jax.shard_map(
-        per_device,
+        functools.partial(per_device, mesh.shape["tx"], mesh.shape["ty"]),
         mesh=mesh,
         in_specs=(P(None, ("tx", "ty"), None), P(), P(), P(), P(), lines, lines, lines, lines,
                   tiles, tiles, tiles, tiles),

time: 99.4 us -> 59 us (0.59); the launches traced: 97.9 us -> 58.6 us
  starting transfers between devices: 29.2 us -> 0 us
  waiting for transfers between devices: 23 us -> 0 us
  Pallas kernels: 32.7 us -> 53.4 us
  other arithmetic: 5.98 us -> 0.67 us
  local copies, waits for them, and re-layouts: 6.26 us -> 3.85 us
    pallas_call x3 -> x1, Pallas kernels: 32.7 us -> 53.4 us  [per_device(): pl.pallas_call(functools.partial(whole_kernel, n_tx, n_ty), name='assimil...]
    all_to_all x1 -> x0, waiting for transfers between devices: 16.2 us -> none  [per_device(): lax.all_to_all(send, ('tx', 'ty'), split_axis=0, concat_axis=0, tiled=True)]
    ppermute x6 -> x0, starting transfers between devices: 15.8 us -> none  [the longest x3 10.2 us: shift_pair(): lax.ppermute(lax.slice_in_dim(x, length - width, length, axis=dim), axis,...]
    all_to_all x1 -> x0, starting transfers between devices: 13.3 us -> none  [per_device(): lax.all_to_all(send, ('tx', 'ty'), split_axis=0, concat_axis=0, tiled=True)]
    ppermute x6 -> x0, waiting for transfers between devices: 6.8 us -> none  [the longest x3 6.8 us: shift_pair(): after = lax.ppermute(lax.slice_in_dim(x, 0, width, axis=dim), axis, down)]
    concatenate x3 -> x0, other arithmetic: 4.56 us -> none  [the longest x1 1.84 us: per_device(): fields = jnp.concatenate([before, fields, after, fill], 2)]
    slice x5 -> x0, local copies, waits for them, and re-layouts: 3.29 us -> none  [the longest x1 1.83 us: per_device(): return (fraction, level[DEPTH:DEPTH + TILE, DEPTH:DEPTH + TILE])]
    unnamed x10 -> x6, local copies, waits for them, and re-layouts: 0.92 us -> 3.73 us
  transfers between devices with their start and end apart: 7 -> 0, of which waited for: 4 -> 0; matrix products, arithmetic and copies ran while one was open for 3% -> 0% of each run, Pallas kernels for 0% -> 0%
where the time goes in v2:
time: 59 us; the launch traced here: 58.6 us
  Pallas kernels  53.4 us (91%)
  local copies, waits for them, and re-layouts  3.85 us (7%)
  other arithmetic  0.67 us (1%)
  between operations  0.66 us (1%)
    pallas_call x1, Pallas kernels, per_device(): pl.pallas_call(functools.partial(whole_kernel, n_tx, n_ty), name='assimil...  53.4 us
    unnamed x6, local copies, waits for them, and re-layouts  3.73 us

profile of v2, /device:TPU:1, one launch (start us, length us, event | category | flops | bytes accessed | tf_op | source)
XLA Modules:
  0.0 58.6 jit_solution(1282680272719683279)
XLA Ops:
  0.6 0.0 copy-start.1
  0.7 0.0 copy-start
  0.7 0.1 pad.2.clone
  0.7 0.6 copy-done.1
  1.3 0.0 copy-done
  1.4 0.7 %maximum_maximum_fusion.refs_1_ = bf16[32,16]{1,0:T(8,128)(2,1)} fusion(bf16[9,16]{1,0:T(8,128)(2,1)S(1)} %reshape.23, bf16[18,16]{1,0:T(8,128)(2,1)S(1)} %reshape.22, bf16[32]{0:T(256)(128)(2,1)S(1)} %pad.2.clone), kind=kLoop, calls=%fused_computation | loop fusion | flops 3072 | bytes 1952 | tf_op jit(solution)/shard_map/concatenate | solution.py:457
  2.0 53.4 %assimilate.1 = (bf16[64,512]{1,0:T(8,128)(2,1)}, f32[256,256]{1,0:T(8,128)}) custom-call(bf16[2,64,512]{2,1,0:T(8,128)(2,1)} %refs_0_.1, bf16[32,16]{1,0:T(8,128)(2,1)} %maximum_maximum_fusion.refs_1_, bf16[144,16]{1,0:T(8,128)(2,1)} %bitcast.10, bf16[144,16]{1,0:T(8,128)(2,1)} %bitcast.11, f32[64,512]{1,0:T(8,128)} %refs_4_.1, s32[64,512]{1,0:T(8,128)} %refs_5_.1, ...), custom_call_target="tpu_custom_call" | custom-call | tf_op jit(solution)/shard_map/assimilate/pallas_call | solution.py:478
  55.5 1.5 %copy.17 = bf16[64,512]{1,0:T(8,128)(2,1)} copy(bf16[64,512]{1,0:T(8,128)(2,1)} %get-tuple-element.4) | data formatting | bytes 131072
  56.9 1.7 %copy.18 = f32[256,256]{1,0:T(8,128)} copy(f32[256,256]{1,0:T(8,128)} %get-tuple-element.5) | data formatting | bytes 524288
  (3 shorter events, 0.0 us)
Async XLA Ops:
  0.6 0.7 %copy-start.1 = (bf16[1,16,3,3]{1,3,2,0:T(4,128)(2,1)S(1)}, bf16[1,16,3,3]{1,3,2,0:T(4,128)(2,1)}, u32[]{:S(2)}) copy-start(bf16[1,16,3,3]{1,3,2,0:T(4,128)(2,1)} %param.17) | copy-start | bytes 868
  0.7 0.7 %copy-start = (bf16[16,2,3,3]{0,1,3,2:T(2,128)(2,1)S(1)}, bf16[16,2,3,3]{0,1,3,2:T(2,128)(2,1)}, u32[]{:S(2)}) copy-start(bf16[16,2,3,3]{0,1,3,2:T(2,128)(2,1)} %param.14) | copy-start | bytes 1732

commit v3 on v2

--- a/solution.py
+++ b/solution.py
@@ -1,4 +1,5 @@
 import functools
+import random
 
 import jax
 import jax.numpy as jnp
@@ -31,6 +32,7 @@
 CORNERS = ((1, 1), (1, -1), (-1, 1), (-1, -1))
 
 MESH = pl.DeviceIdType.MESH
+LOGICAL = pl.DeviceIdType.LOGICAL
 NN = (((1,), (0,)), ((), ()))
 NT = (((1,), (1,)), ((), ()))
 TN = (((0,), (0,)), ((), ()))
@@ -103,41 +105,58 @@
             h_ref[:, start * 16 : (start + width) * 16, :] = jnp.zeros((3, width * 16, PX), BF16)
 
 
-def conv_layers(x_ref, side_ref, xs_ref, w1_ref, w2_ref, w3_ref, ha_ref, hb_ref, first, last):
+def image_rows(xs_ref, pol, at, value):
+    base = pol * IMG_ROWS + at
+    rows = value.shape[0]
+    xs_ref[1, base : base + rows, :] = value
+    xs_ref[0, base : base + rows, :] = shifted(value, 1)
+    xs_ref[2, base : base + rows, :] = shifted(value, -1)
+
+
+def first_block(block, xs_ref, w1_ref, ha_ref):
+    pieces = []
+    for dx in range(3):
+        for pol in range(2):
+            at = pol * IMG_ROWS + block * 16
+            pieces.append(xs_ref[dx, at : at + 32, :].astype(BF16))
+    value = dot(w1_ref[...], jnp.concatenate(pieces, 0))
+    put_rows(ha_ref, block * 256, jnp.maximum(value, 0.0))
+
+
+def wide_block(block, w_ref, src, dst):
+    at = block * 224
+    value = dot(w_ref[0], src[0, at : at + 256, :])
+    value = value + dot(w_ref[1], src[1, at : at + 256, :])
+    value = value + dot(w_ref[2], src[2, at : at + 256, :])
+    put_rows(dst, at, jnp.maximum(value, 0.0))
+
+
+def conv_inside(x_ref, xs_ref, w1_ref, w2_ref, ha_ref, hb_ref):
     for pol in range(2):
-        before = jnp.where(first, 0.0, side_ref[0, pol].astype(F32))
-        after = jnp.where(last, 0.0, side_ref[1, pol].astype(F32))
-        fill = jnp.zeros((IMG_ROWS - AZ - 2 * SIDE, PX), F32)
-        value = jnp.concatenate([before, x_ref[pol].astype(F32), after, fill], 0)
-        base = pol * IMG_ROWS
-        xs_ref[1, base : base + IMG_ROWS, :] = value.astype(BF16)
-        xs_ref[0, base : base + IMG_ROWS, :] = shifted(value, 1).astype(BF16)
-        xs_ref[2, base : base + IMG_ROWS, :] = shifted(value, -1).astype(BF16)
-    for block in range(5):
-        pieces = []
-        for dx in range(3):
-            for pol in range(2):
-                at = pol * IMG_ROWS + block * 16
-                pieces.append(xs_ref[dx, at : at + 32, :])
-        value = dot(w1_ref[...], jnp.concatenate(pieces, 0))
-        put_rows(ha_ref, block * 256, jnp.maximum(value, 0.0))
+        image_rows(xs_ref, pol, SIDE, x_ref[pol].astype(F32))
+        fill = IMG_ROWS - AZ - 2 * SIDE
+        at = pol * IMG_ROWS + AZ + 2 * SIDE
+        xs_ref[:, at : at + fill, :] = jnp.zeros((3, fill, PX), F32)
+    for block in (1, 2, 3):
+        first_block(block, xs_ref, w1_ref, ha_ref)
+    for block in (2, 3):
+        wide_block(block, w2_ref, ha_ref, hb_ref)
+
+
+def conv_rest(side_ref, xs_ref, w1_ref, w2_ref, w3_ref, ha_ref, hb_ref, first, last):
+    for pol in range(2):
+        image_rows(xs_ref, pol, 0, jnp.where(first, 0.0, side_ref[0, pol].astype(F32)))
+        image_rows(xs_ref, pol, SIDE + AZ, jnp.where(last, 0.0, side_ref[1, pol].astype(F32)))
+    for block in (0, 4):
+        first_block(block, xs_ref, w1_ref, ha_ref)
     clear_rows(ha_ref, first, last, 70, 3)
     hb_ref[:, 70 * 16 : 72 * 16, :] = jnp.zeros((3, 32, PX), BF16)
-    for w_ref, src, dst, rows, width in (
-        (w2_ref, ha_ref, hb_ref, 68, 2),
-        (w3_ref, hb_ref, ha_ref, 66, 1),
-    ):
-
-        def block_body(block, carry):
-            at = pl.multiple_of(block * 224, 32)
-            value = dot(w_ref[0], src[0, pl.ds(at, 256), :])
-            value = value + dot(w_ref[1], src[1, pl.ds(at, 256), :])
-            value = value + dot(w_ref[2], src[2, pl.ds(at, 256), :])
-            put_rows(dst, at, jnp.maximum(value, 0.0))
-            return carry
-
-        lax.fori_loop(0, 5, block_body, 0)
-        clear_rows(dst, first, last, rows, width)
+    for block in (0, 1, 4):
+        wide_block(block, w2_ref, ha_ref, hb_ref)
+    clear_rows(hb_ref, first, last, 68, 2)
+    for block in range(5):
+        wide_block(block, w3_ref, hb_ref, ha_ref)
+    clear_rows(ha_ref, first, last, 66, 1)
 
 
 def last_layer(w4_ref, h_ref, logit_ref):
@@ -172,7 +191,7 @@
         win_ref[pl.ds(pl.multiple_of(step * 8, 8), 8), :] = sums[0:8] + sums[8:16]
         return carry
 
-    lax.fori_loop(0, AZ // 2, pair, 0)
+    lax.fori_loop(0, AZ // 2, pair, 0, unroll=8)
 
 
 def slot_rows(tile_ref, row_ref, pick_ref, mark_ref, devices):
@@ -305,23 +324,30 @@
     return copies
 
 
-def exchange(me, devices, n_ty, sent_ref, got_ref, own_sem, send_sem, recv_sem):
+def peers_of(tx, ty):
+    z, x, y, core = lax.div(tx, 4), lax.rem(tx, 4), lax.div(ty, 2), lax.rem(ty, 2)
+    zs = [lax.rem(z + step, 4) * 32 for step in range(4)]
+    xs = [lax.rem(x + step, 4) * 8 for step in range(4)]
+    ys = [lax.rem(y + step, 4) * 2 for step in range(4)]
+    cores = [core, 1 - core]
+    steps = [(a, b, c, d) for a in range(4) for b in range(4) for c in range(4) for d in range(2)]
+    random.Random(3).shuffle(steps)
+    steps.sort(key=lambda step: -sum(min(k, 4 - k) for k in step[:3]))
+    return [zs[a] + xs[b] + ys[c] + cores[d] for a, b, c, d in steps if a or b or c or d]
+
+
+def exchange(me, peers, sent_ref, got_ref, own_sem, send_sem, recv_sem):
     own = pltpu.make_async_copy(sent_ref.at[me], got_ref.at[me], own_sem)
     own.start()
-
-    def send(step, carry):
-        peer = lax.rem(me + step, devices)
+    for peer in peers:
         pltpu.make_async_remote_copy(
             src_ref=sent_ref.at[peer],
             dst_ref=got_ref.at[me],
             send_sem=send_sem,
             recv_sem=recv_sem,
-            device_id=(peer // n_ty, lax.rem(peer, n_ty)),
-            device_id_type=MESH,
+            device_id=peer,
+            device_id_type=LOGICAL,
         ).start()
-        return carry
-
-    lax.fori_loop(1, devices, send, 0)
     return own
 
 
@@ -346,13 +372,9 @@
     place = (tx, ty, n_tx, n_ty)
     barrier = pltpu.get_barrier_semaphore()
 
-    def greet(step, carry):
-        peer = lax.rem(me + step, devices)
-        pl.semaphore_signal(barrier, inc=1, device_id=(peer // n_ty, lax.rem(peer, n_ty)),
-                            device_id_type=MESH)
-        return carry
-
-    lax.fori_loop(1, devices, greet, 0)
+    peers = peers_of(tx, ty)
+    for peer in peers:
+        pl.semaphore_signal(barrier, inc=1, device_id=peer, device_id_type=LOGICAL)
     loads = []
     for number, (src, dst) in enumerate(
         ((slope_in, slope_ref), (rain_in, rain_in_ref), (dir_in, dir_ref), (geo_in, geo_ref),
@@ -370,6 +392,11 @@
     direction = dirs_ref.at[1]
     for index, field in enumerate((conv_ref, rain_ref, direction)):
         fill_edges(field, index, rows_s, cols_s, corners_s)
+    line_sums(geo_ref, cell_ref, win_ref)
+    covered = jnp.concatenate([win_ref[...].astype(BF16), mark_ref[...]], 1)
+    placed = dot(pick_ref[...], covered)
+    early_ref[:, 0:8, :] = placed[:, 0:128].reshape(devices, 8, 128).astype(BF16)
+    early_ref[:, 8:16, :] = placed[:, 128:256].reshape(devices, 8, 128).astype(BF16)
     pl.semaphore_wait(barrier, devices - 1)
 
     sides = []
@@ -390,17 +417,12 @@
                         edge_send, edge_recv)
     for copy in edges:
         copy.start()
-    line_sums(geo_ref, cell_ref, win_ref)
-    covered = jnp.concatenate([win_ref[...].astype(BF16), mark_ref[...]], 1)
-    placed = dot(pick_ref[...], covered)
-    early_ref[:, 0:8, :] = placed[:, 0:128].reshape(devices, 8, 128).astype(BF16)
-    early_ref[:, 8:16, :] = placed[:, 128:256].reshape(devices, 8, 128).astype(BF16)
-    own_early = exchange(me, devices, n_ty, early_ref, early_got, own_sem.at[0], early_send, early_recv)
-
+    own_early = exchange(me, peers, early_ref, early_got, own_sem.at[0], early_send, early_recv)
+
+    conv_inside(x_ref, xs_ref, w1_ref, w2_ref, ha_ref, hb_ref)
     for copy in sides:
         copy.wait()
-    conv_layers(x_ref, side_ref, xs_ref, w1_ref, w2_ref, w3_ref, ha_ref, hb_ref,
-                me == 0, me == devices - 1)
+    conv_rest(side_ref, xs_ref, w1_ref, w2_ref, w3_ref, ha_ref, hb_ref, me == 0, me == devices - 1)
     last_layer(w4_ref, ha_ref, logit_ref)
     fraction = (1.0 / (1.0 + jnp.exp(-logit_ref[...]))).astype(BF16)
     frac_ref[...] = fraction
@@ -408,7 +430,7 @@
     line_sums(logit_ref, cell_ref, win_ref)
     placed = dot(pick_ref[...], win_ref[...].astype(BF16))
     late_ref[...] = placed.reshape(devices, 8, 128).astype(BF16)
-    own_late = exchange(me, devices, n_ty, late_ref, late_got, own_sem.at[1], late_send, late_recv)
+    own_late = exchange(me, peers, late_ref, late_got, own_sem.at[1], late_send, late_recv)
 
     for copy in edges:
         copy.wait()
@@ -498,7 +520,7 @@
             pltpu.VMEM((3, 224, 256), BF16),
             pltpu.VMEM((24, 256), F32),
             pltpu.VMEM((2, 2, SIDE, PX), BF16),
-            pltpu.VMEM((3, 2 * IMG_ROWS, PX), BF16),
+            pltpu.VMEM((3, 2 * IMG_ROWS, PX), F32),
             pltpu.VMEM((3, ROWS1 * 16, PX), BF16),
             pltpu.VMEM((3, ROWS1 * 16, PX), BF16),
             pltpu.VMEM((AZ, PX), F32),

time: 59 us -> 46.5 us (0.79)
  Pallas kernels: 53.4 us -> 41 us
    pallas_call x1, Pallas kernels: 53.4 us -> 41 us  [per_device(): pl.pallas_call(functools.partial(whole_kernel, n_tx, n_ty), name='assimil...]
where the time goes in v3:
time: 46.5 us; the launch traced here: 46.1 us
  Pallas kernels  41 us (88%)
  local copies, waits for them, and re-layouts  3.85 us (8%)
  other arithmetic  0.67 us (1%)
  between operations  0.66 us (1%)
    pallas_call x1, Pallas kernels, per_device(): pl.pallas_call(functools.partial(whole_kernel, n_tx, n_ty), name='assimil...  41 us
    unnamed x6, local copies, waits for them, and re-layouts  3.73 us

profile of v3, /device:TPU:1, one launch (start us, length us, event | category | flops | bytes accessed | tf_op | source)
XLA Modules:
  0.0 46.1 jit_solution(15920155807991178904)
XLA Ops:
  0.6 0.0 copy-start.1
  0.7 0.0 copy-start
  0.7 0.1 pad.2.clone
  0.7 0.6 %copy-done.1 = bf16[1,16,3,3]{1,3,2,0:T(4,128)(2,1)S(1)} copy-done((bf16[1,16,3,3]{1,3,2,0:T(4,128)(2,1)S(1)}, bf16[1,16,3,3]{1,3,2,0:T(4,128)(2,1)}, u32[]{:S(2)}) %copy-start.1) | copy-done | bytes 312
  1.3 0.0 copy-done
  1.4 0.7 %maximum_maximum_fusion.refs_1_ = bf16[32,16]{1,0:T(8,128)(2,1)} fusion(bf16[9,16]{1,0:T(8,128)(2,1)S(1)} %reshape.23, bf16[18,16]{1,0:T(8,128)(2,1)S(1)} %reshape.22, bf16[32]{0:T(256)(128)(2,1)S(1)} %pad.2.clone), kind=kLoop, calls=%fused_computation | loop fusion | flops 3072 | bytes 1952 | tf_op jit(solution)/shard_map/concatenate | solution.py:479
  2.0 41.0 %assimilate.1 = (bf16[64,512]{1,0:T(8,128)(2,1)}, f32[256,256]{1,0:T(8,128)}) custom-call(bf16[2,64,512]{2,1,0:T(8,128)(2,1)} %refs_0_.1, bf16[32,16]{1,0:T(8,128)(2,1)} %maximum_maximum_fusion.refs_1_, bf16[144,16]{1,0:T(8,128)(2,1)} %bitcast.10, bf16[144,16]{1,0:T(8,128)(2,1)} %bitcast.11, f32[64,512]{1,0:T(8,128)} %refs_4_.1, s32[64,512]{1,0:T(8,128)} %refs_5_.1, ...), custom_call_target="tpu_custom_call" | custom-call | tf_op jit(solution)/shard_map/assimilate/pallas_call | solution.py:500
  43.0 1.5 %copy.17 = bf16[64,512]{1,0:T(8,128)(2,1)} copy(bf16[64,512]{1,0:T(8,128)(2,1)} %get-tuple-element.4) | data formatting | bytes 131072
  44.5 1.7 %copy.18 = f32[256,256]{1,0:T(8,128)} copy(f32[256,256]{1,0:T(8,128)} %get-tuple-element.5) | data formatting | bytes 524288
  (3 shorter events, 0.0 us)
Async XLA Ops:
  0.6 0.7 %copy-start.1 = (bf16[1,16,3,3]{1,3,2,0:T(4,128)(2,1)S(1)}, bf16[1,16,3,3]{1,3,2,0:T(4,128)(2,1)}, u32[]{:S(2)}) copy-start(bf16[1,16,3,3]{1,3,2,0:T(4,128)(2,1)} %param.17) | copy-start | bytes 868
  0.7 0.7 %copy-start = (bf16[16,2,3,3]{0,1,3,2:T(2,128)(2,1)S(1)}, bf16[16,2,3,3]{0,1,3,2:T(2,128)(2,1)}, u32[]{:S(2)}) copy-start(bf16[16,2,3,3]{0,1,3,2:T(2,128)(2,1)} %param.14) | copy-start | bytes 1732
